TPU v7x, 512 devices: a whole 4x4x16 slice. The times are simulated.
512 devices in a mesh: sec: 2 (over z_hi), gx: 32 (over z_lo, x), row: 8 (over y, core).
Axes of the slice: x: 4, y: 4, z: 16 (z_hi: 2, z_lo: 8; z = z_hi * 8 + z_lo), core: 2. Of those that a mesh axis runs over, the one named last changes fastest.
Arguments:
- fields: float32 [2, 5, 256, 64, 128], P('sec', None, 'gx', 'row'), may hold values from -1.25 to 5, as said below
- mean_flow: float32 [5, 256, 64, 128], P(None, 'gx', 'row'), may hold values from -1 to 1.4, as said below
- source_blocks: int32 [64], replicated, may hold values 0 or 1
Outputs:
- fields_out: float32 [2, 5, 256, 64, 128], P('sec', None, 'gx', 'row')
Inputs may be any that keep to these rules, and one draw needn't show every extreme that they name: `fields`: section 0 holds density in 0.8 to 1.25, momenta of velocities within -1 to 1 and total energy of a pressure in 0.8 to 1.25; section 1 holds perturbations within -1 to 1. `mean_flow`: mean velocities lie within -1 to 1, mean density in 0.8 to 1.25 and sound speed in 0.7 to 1.4.
All inputs are finite; a program needn't handle non-finite values.
Results may differ from a plain program's by a relative error of at most 0.0001.
Values sent between devices are 32-bit elements; how exact they have to be, the bound alone decides.
A program may use at most 64 MiB of HBM per device.

v0:
```python
import jax
import jax.numpy as jnp
from jax import lax
from jax.sharding import PartitionSpec as P

MBLEN = 4


GAMMA = 1.4
STEP_DT = 0.2
VISCOSITY = 0.05


def extended(value, sides, width):
    edges = {}
    for axis, dim in sides:
        size, length = (lax.axis_size(axis), value.shape[dim])
        up = [(i, (i + 1) % size) for i in range(size)]
        last = lax.slice_in_dim(value, length - width, length, axis=dim)
        leading = lax.slice_in_dim(value, 0, width, axis=dim)
        edges[dim] = (
            lax.ppermute(last, axis, up),
            lax.ppermute(leading, axis, [(b, a) for a, b in up]),
        )
    done = []
    for _, dim in sides:
        low, high = edges[dim]
        around = [(width, width) if d in done else (0, 0) for d in range(value.ndim)]
        value = jnp.concatenate([jnp.pad(low, around), value, jnp.pad(high, around)], axis=dim)
        done.append(dim)
    return value


def from_behind(value, axis, steps):
    count = lax.axis_size(axis)
    leading, last = (max(0, -steps), min(count, count - steps))
    return lax.ppermute(value, axis, [(source, source + steps) for source in range(leading, last)])


def offset_cells(values, direction, shift_by):
    length_x = values.shape[-3]
    length_y = values.shape[-2]
    if direction == 2:
        return jnp.roll(values[..., 2 : length_x - 2, 2 : length_y - 2, :], -shift_by, axis=-1)
    if direction == 0:
        return values[..., 2 + shift_by : length_x - 2 + shift_by, 2 : length_y - 2, :]
    return values[..., 2 : length_x - 2, 2 + shift_by : length_y - 2 + shift_by, :]


def central_first(values, direction):
    return (
        8.0 * (offset_cells(values, direction, 1) - offset_cells(values, direction, -1))
        - (offset_cells(values, direction, 2) - offset_cells(values, direction, -2))
    ) / 12.0


def central_second(values, direction):
    return (
        -offset_cells(values, direction, 2)
        + 16.0 * offset_cells(values, direction, 1)
        - 30.0 * offset_cells(values, direction, 0)
        + 16.0 * offset_cells(values, direction, -1)
        - offset_cells(values, direction, -2)
    ) / 12.0


def trim_rim(values, amount):
    if amount == 0:
        return values
    return values[..., amount:-amount, amount:-amount, :]


def flow_rate(padded):
    density = padded[0]
    momentum = padded[1:4]
    energy = padded[4]
    velocity = momentum / density
    pressure = (GAMMA - 1.0) * (energy - 0.5 * jnp.sum(momentum * velocity, axis=0))
    total = None
    for direction in range(3):
        along = velocity[direction]
        unit_vector = jnp.zeros((3,), jnp.float32).at[direction].set(1.0)
        middle = momentum * along[None] + pressure[None] * unit_vector[:, None, None, None]
        flux = jnp.concatenate(
            [momentum[direction][None], middle, ((energy + pressure) * along)[None]], axis=0
        )
        term = -central_first(flux, direction)
        total = term if total is None else total + term
    spread = central_second(padded, 0) + central_second(padded, 1) + central_second(padded, 2)
    return total + VISCOSITY * spread


def lamb_vector(velocity):
    interior = trim_rim(velocity, 2)
    spin_first = central_first(velocity[2], 1) - central_first(velocity[1], 2)
    spin_second = central_first(velocity[0], 2) - central_first(velocity[2], 0)
    spin_third = central_first(velocity[1], 0) - central_first(velocity[0], 1)
    return jnp.stack(
        [
            spin_second * interior[2] - spin_third * interior[1],
            spin_third * interior[0] - spin_first * interior[2],
            spin_first * interior[1] - spin_second * interior[0],
        ]
    )


def acoustic_rate(padded, mean_here, source):
    mean_velocity = mean_here[0:3]

    def convect(values):
        return (
            mean_velocity[0] * central_first(values, 0)
            + mean_velocity[1] * central_first(values, 1)
            + mean_velocity[2] * central_first(values, 2)
        )

    divergence = (
        central_first(padded[1], 0) + central_first(padded[2], 1) + central_first(padded[3], 2)
    )
    density_rate = -convect(padded[0]) - mean_here[3] * divergence
    velocity_rates = [
        -convect(padded[1 + component])
        - central_first(padded[4], component) / mean_here[3]
        - source[component]
        for component in range(3)
    ]
    pressure_rate = -convect(padded[4]) - mean_here[3] * mean_here[4] * mean_here[4] * divergence
    return jnp.stack([density_rate] + velocity_rates + [pressure_rate])


def widen_state(values):
    return extended(values, (("gx", 1), ("row", 2)), 2)


def local(fields, mean_flow, source_blocks):
    state = fields[0]
    is_flow = lax.axis_index("sec") == 0
    extent_x = state.shape[1]
    blocks_total = source_blocks.shape[0]
    global_x = extent_x * lax.axis_size("gx")
    outer_rim = 2
    mean_rim = 0
    lamb_rim = outer_rim - 2
    row_index = (
        lax.axis_index("gx") * extent_x
        + jnp.arange(extent_x + 2 * lamb_rim, dtype=jnp.int32)
        - lamb_rim
    )
    row_index = jnp.mod(row_index, global_x)
    block_ids = row_index // MBLEN
    lookup_table = (
        block_ids[:, None] == jnp.arange(blocks_total, dtype=jnp.int32)[None, :]
    ).astype(jnp.float32)
    mask_rows = jnp.dot(
        lookup_table, source_blocks.astype(jnp.float32), precision=lax.Precision.HIGHEST
    )
    padded = widen_state(state)
    lamb_shape = (3, padded.shape[1] - 4, padded.shape[2] - 4, padded.shape[3])
    lamb_field = lax.cond(
        is_flow,
        lambda: lamb_vector(padded[1:4] / padded[0]),
        lambda: jnp.zeros(lamb_shape, jnp.float32),
    )
    arrived = from_behind(lamb_field, "sec", 1)
    source = arrived * mask_rows[None, :, None, None]

    def section_rate(values, out_rim):
        mean_here = trim_rim(mean_flow, mean_rim - out_rim)
        source_here = trim_rim(source, lamb_rim - out_rim)
        return lax.cond(
            is_flow,
            lambda: flow_rate(values),
            lambda: acoustic_rate(values, mean_here, source_here),
        )

    slope_one = section_rate(padded, 0)
    slope_two = section_rate(widen_state(state + 0.5 * STEP_DT * slope_one), 0)
    slope_three = section_rate(widen_state(state + 0.5 * STEP_DT * slope_two), 0)
    slope_four = section_rate(widen_state(state + STEP_DT * slope_three), 0)
    state = state + STEP_DT / 6.0 * (slope_one + 2.0 * slope_two + 2.0 * slope_three + slope_four)
    return state[None]


def solution(mesh):
    placed = (P("sec", None, "gx", "row", None), P(None, "gx", "row", None), P())
    return jax.shard_map(
        local,
        mesh=mesh,
        in_specs=placed,
        out_specs=P("sec", None, "gx", "row", None),
        check_vma=False,
    )
```

profile of v0, /device:TPU:25, one launch (start us, length us, event | category | flops | bytes accessed | tf_op | source)
XLA Modules:
  0.0 107.8 jit_solution(147466299929129830)
XLA Ops:
  0.0 0.9 fusion.620
  0.9 3.1 %collective-permute-start.1 = (f32[5,2,8,128]{3,2,1,0:T(8,128)S(1)}, f32[5,2,8,128]{3,2,1,0:T(8,128)S(1)}, u32[]{:S(2)}, u32[]{:S(2)}) collective-permute-start(f32[5,2,8,128]{3,2,1,0:T(8,128)S(1)} %get-tuple-element.729), channel_id=1, source_target_pairs={{0,8},{8,16},{16,24},{24,32},{32,40},{40,48},{48,56},{56,64},{64,7... | collective-permute-start | bytes 122888 | tf_op jit(solution)/shard_map/ppermute | solution.py:22
  4.0 13.9 %collective-permute-start.2 = (f32[5,2,8,128]{3,2,1,0:T(8,128)S(1)}, f32[5,2,8,128]{3,2,1,0:T(8,128)S(1)}, u32[]{:S(2)}, u32[]{:S(2)}) collective-permute-start(f32[5,2,8,128]{3,2,1,0:T(8,128)S(1)} %get-tuple-element.730), channel_id=1, source_target_pairs={{8,0},{16,8},{24,16},{32,24},{40,32},{48,40},{56,48},{64,56},{72,6... | collective-permute-start | bytes 122888 | tf_op jit(solution)/shard_map/ppermute | solution.py:23
  17.9 3.4 %collective-permute-start = (f32[5,8,2,128]{3,2,1,0:T(2,128)S(1)}, f32[5,8,2,128]{3,2,1,0:T(2,128)S(1)}, u32[]{:S(2)}, u32[]{:S(2)}) collective-permute-start(f32[5,8,2,128]{3,2,1,0:T(2,128)S(1)} %get-tuple-element.731), channel_id=1, source_target_pairs={{0,1},{1,2},{2,3},{3,4},{4,5},{5,6},{6,7},{7,0},{8,9},{9,10},{10,1... | collective-permute-start | bytes 122888 | tf_op jit(solution)/shard_map/ppermute | solution.py:22
  21.4 0.6 copy-done.14
  22.0 0.2 convolution_bitcast_fusion
  22.2 0.2 collective-permute-done
  22.4 3.5 %collective-permute-done.3 = f32[5,8,2,128]{3,2,1,0:T(2,128)S(1)} collective-permute-done((f32[5,8,2,128]{3,2,1,0:T(2,128)S(1)}, f32[5,8,2,128]{3,2,1,0:T(2,128)S(1)}, u32[]{:S(2)}, u32[]{:S(2)}) %collective-permute-start.3) | collective-permute-done | bytes 40992 | tf_op jit(solution)/shard_map/ppermute | solution.py:23
  26.1 0.7 conditional.5
  26.5 0.1 subtract_bitcast_fusion.2
  26.6 0.1 subtract_bitcast_fusion.1
  26.8 9.4 %collective-permute-start.4 = (f32[3,8,8,128]{3,2,1,0:T(8,128)S(1)}, f32[3,8,8,128]{3,2,1,0:T(8,128)S(1)}, u32[]{:S(2)}, u32[]{:S(2)}) collective-permute-start(f32[3,8,8,128]{3,2,1,0:T(8,128)S(1)} %get-tuple-element.733), channel_id=1, source_target_pairs={{0,256},{1,257},{2,258},{3,259},{4,260},{5,261},{6,262},{7,263},{8... | collective-permute-start | bytes 294920 | tf_op jit(solution)/shard_map/ppermute | solution.py:37
  36.2 2.0 %collective-permute-done.4 = f32[3,8,8,128]{3,2,1,0:T(8,128)S(1)} collective-permute-done((f32[3,8,8,128]{3,2,1,0:T(8,128)S(1)}, f32[3,8,8,128]{3,2,1,0:T(8,128)S(1)}, u32[]{:S(2)}, u32[]{:S(2)}) %collective-permute-start.4) | collective-permute-done | bytes 98336 | tf_op jit(solution)/shard_map/ppermute | solution.py:37
  38.3 2.4 %conditional.6 = (f32[5,8,8,128]{3,2,1,0:T(8,128)S(1)}) conditional(s32[]{:T(128)} %convert_element_type.20, (f32[5,8,8,128]{3,2,1,0:T(8,128)S(1)}, f32[5,12,12,128]{3,2,1,0:T(8,128)S(1)}, f32[3,8,8,128]{3,2,1,0:T(8,128)S(1)}) %tuple.431, (f32[5,12,12,128]{3,2,1,0:T(8,128)S(1)}, f32[5,12,8,128]{3,2,1,0:T(8,128)S(1)}, ...), branch_computations={%region_2.3_spmd, %region_3.5_spmd} | conditional | flops 3538944 | bytes 12337424 | solution.py:170
  38.4 0.1 slice_multiply_fusion
  38.5 0.6 copy-done.2
  39.2 0.2 multiply_add_fusion
  39.5 0.2 fusion.525
  39.6 0.2 fusion.524
  39.8 0.2 fusion.523
  40.0 0.2 fusion.522
  40.1 0.6 fusion.114
  40.8 1.9 %collective-permute-start.6 = (f32[5,2,8,128]{3,2,1,0:T(8,128)S(1)}, f32[5,2,8,128]{3,2,1,0:T(8,128)S(1)}, u32[]{:S(2)}, u32[]{:S(2)}) collective-permute-start(f32[5,2,8,128]{3,2,1,0:T(8,128)S(1)} %get-tuple-element.725), channel_id=1, source_target_pairs={{0,8},{8,16},{16,24},{24,32},{32,40},{40,48},{48,56},{56,64},{64,7... | collective-permute-start | bytes 122888 | tf_op jit(solution)/shard_map/ppermute | solution.py:22
  42.7 12.1 %collective-permute-start.7 = (f32[5,2,8,128]{3,2,1,0:T(8,128)S(1)}, f32[5,2,8,128]{3,2,1,0:T(8,128)S(1)}, u32[]{:S(2)}, u32[]{:S(2)}) collective-permute-start(f32[5,2,8,128]{3,2,1,0:T(8,128)S(1)} %get-tuple-element.726), channel_id=1, source_target_pairs={{8,0},{16,8},{24,16},{32,24},{40,32},{48,40},{56,48},{64,56},{72,6... | collective-permute-start | bytes 122888 | tf_op jit(solution)/shard_map/ppermute | solution.py:23
  54.8 1.5 %collective-permute-start.5 = (f32[5,8,2,128]{3,2,1,0:T(2,128)S(1)}, f32[5,8,2,128]{3,2,1,0:T(2,128)S(1)}, u32[]{:S(2)}, u32[]{:S(2)}) collective-permute-start(f32[5,8,2,128]{3,2,1,0:T(2,128)S(1)} %get-tuple-element.727), channel_id=1, source_target_pairs={{0,1},{1,2},{2,3},{3,4},{4,5},{5,6},{6,7},{7,0},{8,9},{9,10},{10,1... | collective-permute-start | bytes 122888 | tf_op jit(solution)/shard_map/ppermute | solution.py:22
  56.3 1.1 %collective-permute-done.5 = f32[5,8,2,128]{3,2,1,0:T(2,128)S(1)} collective-permute-done((f32[5,8,2,128]{3,2,1,0:T(2,128)S(1)}, f32[5,8,2,128]{3,2,1,0:T(2,128)S(1)}, u32[]{:S(2)}, u32[]{:S(2)}) %collective-permute-start.5) | collective-permute-done | bytes 40992 | tf_op jit(solution)/shard_map/ppermute | solution.py:22
  57.4 3.5 %collective-permute-done.8 = f32[5,8,2,128]{3,2,1,0:T(2,128)S(1)} collective-permute-done((f32[5,8,2,128]{3,2,1,0:T(2,128)S(1)}, f32[5,8,2,128]{3,2,1,0:T(2,128)S(1)}, u32[]{:S(2)}, u32[]{:S(2)}) %collective-permute-start.8) | collective-permute-done | bytes 40992 | tf_op jit(solution)/shard_map/ppermute | solution.py:23
  61.1 2.4 %conditional.7 = (f32[5,8,8,128]{3,2,1,0:T(8,128)S(1)}) conditional(s32[]{:T(128)} %convert_element_type.20, (f32[5,8,8,128]{3,2,1,0:T(8,128)S(1)}, f32[5,12,12,128]{3,2,1,0:T(8,128)S(1)}, f32[3,8,8,128]{3,2,1,0:T(8,128)S(1)}) %tuple.432, (f32[5,12,12,128]{3,2,1,0:T(8,128)S(1)}, f32[5,12,8,128]{3,2,1,0:T(8,128)S(1)}, ...), branch_computations={%region_5.6_spmd, %region_6.8_spmd} | conditional | flops 3538944 | bytes 12337424 | solution.py:170
  61.3 0.6 copy-done.3
  61.9 0.2 multiply_add_fusion.3
  62.2 0.2 fusion.553
  62.4 0.2 fusion.552
  62.6 0.2 fusion.551
  62.7 0.2 fusion.550
  62.9 0.6 fusion.225
  63.5 1.9 %collective-permute-start.10 = (f32[5,2,8,128]{3,2,1,0:T(8,128)S(1)}, f32[5,2,8,128]{3,2,1,0:T(8,128)S(1)}, u32[]{:S(2)}, u32[]{:S(2)}) collective-permute-start(f32[5,2,8,128]{3,2,1,0:T(8,128)S(1)} %get-tuple-element.721), channel_id=1, source_target_pairs={{0,8},{8,16},{16,24},{24,32},{32,40},{40,48},{48,56},{56,64},{64,7... | collective-permute-start | bytes 122888 | tf_op jit(solution)/shard_map/ppermute | solution.py:22
  65.5 12.1 %collective-permute-start.11 = (f32[5,2,8,128]{3,2,1,0:T(8,128)S(1)}, f32[5,2,8,128]{3,2,1,0:T(8,128)S(1)}, u32[]{:S(2)}, u32[]{:S(2)}) collective-permute-start(f32[5,2,8,128]{3,2,1,0:T(8,128)S(1)} %get-tuple-element.722), channel_id=1, source_target_pairs={{8,0},{16,8},{24,16},{32,24},{40,32},{48,40},{56,48},{64,56},{72,6... | collective-permute-start | bytes 122888 | tf_op jit(solution)/shard_map/ppermute | solution.py:23
  77.5 0.6 collective-permute-start.9
  78.1 0.5 collective-permute-done.11
  78.6 0.6 collective-permute-done.9
  79.2 3.5 %collective-permute-done.12 = f32[5,8,2,128]{3,2,1,0:T(2,128)S(1)} collective-permute-done((f32[5,8,2,128]{3,2,1,0:T(2,128)S(1)}, f32[5,8,2,128]{3,2,1,0:T(2,128)S(1)}, u32[]{:S(2)}, u32[]{:S(2)}) %collective-permute-start.12) | collective-permute-done | bytes 40992 | tf_op jit(solution)/shard_map/ppermute | solution.py:23
  82.9 2.4 %conditional.8 = (f32[5,8,8,128]{3,2,1,0:T(8,128)S(1)}) conditional(s32[]{:T(128)} %convert_element_type.20, (f32[5,8,8,128]{3,2,1,0:T(8,128)S(1)}, f32[5,12,12,128]{3,2,1,0:T(8,128)S(1)}, f32[3,8,8,128]{3,2,1,0:T(8,128)S(1)}) %tuple.433, (f32[5,12,12,128]{3,2,1,0:T(8,128)S(1)}, f32[5,12,8,128]{3,2,1,0:T(8,128)S(1)}, ...), branch_computations={%region_8.9_spmd, %region_9.11_spmd} | conditional | flops 3538944 | bytes 12337424 | solution.py:170
  83.1 0.6 copy-done.4
  83.7 0.2 multiply_add_fusion.6
  84.1 0.2 fusion.581
  84.2 0.2 fusion.580
  84.4 0.2 fusion.579
  84.5 0.2 fusion.578
  84.7 0.6 fusion.336
  85.4 1.9 %collective-permute-start.14 = (f32[5,2,8,128]{3,2,1,0:T(8,128)S(1)}, f32[5,2,8,128]{3,2,1,0:T(8,128)S(1)}, u32[]{:S(2)}, u32[]{:S(2)}) collective-permute-start(f32[5,2,8,128]{3,2,1,0:T(8,128)S(1)} %get-tuple-element.717), channel_id=1, source_target_pairs={{0,8},{8,16},{16,24},{24,32},{32,40},{40,48},{48,56},{56,64},{64,7... | collective-permute-start | bytes 122888 | tf_op jit(solution)/shard_map/ppermute | solution.py:22
  87.3 12.1 %collective-permute-start.15 = (f32[5,2,8,128]{3,2,1,0:T(8,128)S(1)}, f32[5,2,8,128]{3,2,1,0:T(8,128)S(1)}, u32[]{:S(2)}, u32[]{:S(2)}) collective-permute-start(f32[5,2,8,128]{3,2,1,0:T(8,128)S(1)} %get-tuple-element.718), channel_id=1, source_target_pairs={{8,0},{16,8},{24,16},{32,24},{40,32},{48,40},{56,48},{64,56},{72,6... | collective-permute-start | bytes 122888 | tf_op jit(solution)/shard_map/ppermute | solution.py:23
  99.4 0.6 collective-permute-start.13
  99.9 0.5 collective-permute-done.15
  100.4 0.6 collective-permute-done.13
  101.0 3.5 %collective-permute-done.16 = f32[5,8,2,128]{3,2,1,0:T(2,128)S(1)} collective-permute-done((f32[5,8,2,128]{3,2,1,0:T(2,128)S(1)}, f32[5,8,2,128]{3,2,1,0:T(2,128)S(1)}, u32[]{:S(2)}, u32[]{:S(2)}) %collective-permute-start.16) | collective-permute-done | bytes 40992 | tf_op jit(solution)/shard_map/ppermute | solution.py:23
  104.7 2.4 %conditional.9 = (f32[5,8,8,128]{3,2,1,0:T(8,128)S(1)}) conditional(s32[]{:T(128)} %convert_element_type.20, (f32[5,8,8,128]{3,2,1,0:T(8,128)S(1)}, f32[5,12,12,128]{3,2,1,0:T(8,128)S(1)}, f32[3,8,8,128]{3,2,1,0:T(8,128)S(1)}) %tuple.434, (f32[5,12,12,128]{3,2,1,0:T(8,128)S(1)}, f32[5,12,8,128]{3,2,1,0:T(8,128)S(1)}, ...), branch_computations={%region_11.12_spmd, %region_12.14_spmd} | conditional | flops 3538944 | bytes 12337424 | solution.py:170
  104.9 0.6 copy-done.5
  105.6 0.2 multiply_add_fusion.9
  105.9 0.2 fusion.609
  106.0 0.2 fusion.608
  106.2 0.2 fusion.607
  106.4 0.2 fusion.606
  106.5 0.6 fusion.447
  107.1 0.7 add_bitcast_fusion
  (83 shorter events, 2.2 us)
Async XLA Ops:
  0.0 17.9 %copy-start.1 = (f32[1,5,8,8,128]{4,3,2,1,0:T(8,128)S(1)}, f32[1,5,8,8,128]{4,3,2,1,0:T(8,128)}, u32[]{:S(2)}) copy-start(f32[1,5,8,8,128]{4,3,2,1,0:T(8,128)} %param.37) | copy-start | bytes 491524
  0.9 21.3 %collective-permute-start.1 = (f32[5,2,8,128]{3,2,1,0:T(8,128)S(1)}, f32[5,2,8,128]{3,2,1,0:T(8,128)S(1)}, u32[]{:S(2)}, u32[]{:S(2)}) collective-permute-start(f32[5,2,8,128]{3,2,1,0:T(8,128)S(1)} %get-tuple-element.729), channel_id=1, source_target_pairs={{0,8},{8,16},{16,24},{24,32},{32,40},{40,48},{48,56},{56,64},{64,7... | collective-permute-start | bytes 122888 | tf_op jit(solution)/shard_map/ppermute | solution.py:22
  4.0 18.2 %collective-permute-start.2 = (f32[5,2,8,128]{3,2,1,0:T(8,128)S(1)}, f32[5,2,8,128]{3,2,1,0:T(8,128)S(1)}, u32[]{:S(2)}, u32[]{:S(2)}) collective-permute-start(f32[5,2,8,128]{3,2,1,0:T(8,128)S(1)} %get-tuple-element.730), channel_id=1, source_target_pairs={{8,0},{16,8},{24,16},{32,24},{40,32},{48,40},{56,48},{64,56},{72,6... | collective-permute-start | bytes 122888 | tf_op jit(solution)/shard_map/ppermute | solution.py:23
  17.9 4.5 %collective-permute-start = (f32[5,8,2,128]{3,2,1,0:T(2,128)S(1)}, f32[5,8,2,128]{3,2,1,0:T(2,128)S(1)}, u32[]{:S(2)}, u32[]{:S(2)}) collective-permute-start(f32[5,8,2,128]{3,2,1,0:T(2,128)S(1)} %get-tuple-element.731), channel_id=1, source_target_pairs={{0,1},{1,2},{2,3},{3,4},{4,5},{5,6},{6,7},{7,0},{8,9},{9,10},{10,1... | collective-permute-start | bytes 122888 | tf_op jit(solution)/shard_map/ppermute | solution.py:22
  21.3 4.6 %collective-permute-start.3 = (f32[5,8,2,128]{3,2,1,0:T(2,128)S(1)}, f32[5,8,2,128]{3,2,1,0:T(2,128)S(1)}, u32[]{:S(2)}, u32[]{:S(2)}) collective-permute-start(f32[5,8,2,128]{3,2,1,0:T(2,128)S(1)} %get-tuple-element.732), channel_id=1, source_target_pairs={{1,0},{2,1},{3,2},{4,3},{5,4},{6,5},{7,6},{0,7},{9,8},{10,9},{11,1... | collective-permute-start | bytes 122888 | tf_op jit(solution)/shard_map/ppermute | solution.py:23
  21.3 0.7 copy-start.14
  26.8 11.4 %collective-permute-start.4 = (f32[3,8,8,128]{3,2,1,0:T(8,128)S(1)}, f32[3,8,8,128]{3,2,1,0:T(8,128)S(1)}, u32[]{:S(2)}, u32[]{:S(2)}) collective-permute-start(f32[3,8,8,128]{3,2,1,0:T(8,128)S(1)} %get-tuple-element.733), channel_id=1, source_target_pairs={{0,256},{1,257},{2,258},{3,259},{4,260},{5,261},{6,262},{7,263},{8... | collective-permute-start | bytes 294920 | tf_op jit(solution)/shard_map/ppermute | solution.py:37
  36.2 2.1 %copy-start = (f32[5,8,8,128]{3,2,1,0:T(8,128)S(1)}, f32[5,8,8,128]{3,2,1,0:T(8,128)}, u32[]{:S(2)}) copy-start(f32[5,8,8,128]{3,2,1,0:T(8,128)} %param.38) | copy-start | bytes 491524
  38.5 0.7 copy-start.2
  38.5 0.7 copy-start.6
  38.5 0.7 copy-start.7
  40.8 15.5 %collective-permute-start.6 = (f32[5,2,8,128]{3,2,1,0:T(8,128)S(1)}, f32[5,2,8,128]{3,2,1,0:T(8,128)S(1)}, u32[]{:S(2)}, u32[]{:S(2)}) collective-permute-start(f32[5,2,8,128]{3,2,1,0:T(8,128)S(1)} %get-tuple-element.725), channel_id=1, source_target_pairs={{0,8},{8,16},{16,24},{24,32},{32,40},{40,48},{48,56},{56,64},{64,7... | collective-permute-start | bytes 122888 | tf_op jit(solution)/shard_map/ppermute | solution.py:22
  42.7 13.6 %collective-permute-start.7 = (f32[5,2,8,128]{3,2,1,0:T(8,128)S(1)}, f32[5,2,8,128]{3,2,1,0:T(8,128)S(1)}, u32[]{:S(2)}, u32[]{:S(2)}) collective-permute-start(f32[5,2,8,128]{3,2,1,0:T(8,128)S(1)} %get-tuple-element.726), channel_id=1, source_target_pairs={{8,0},{16,8},{24,16},{32,24},{40,32},{48,40},{56,48},{64,56},{72,6... | collective-permute-start | bytes 122888 | tf_op jit(solution)/shard_map/ppermute | solution.py:23
  54.8 2.6 %collective-permute-start.5 = (f32[5,8,2,128]{3,2,1,0:T(2,128)S(1)}, f32[5,8,2,128]{3,2,1,0:T(2,128)S(1)}, u32[]{:S(2)}, u32[]{:S(2)}) collective-permute-start(f32[5,8,2,128]{3,2,1,0:T(2,128)S(1)} %get-tuple-element.727), channel_id=1, source_target_pairs={{0,1},{1,2},{2,3},{3,4},{4,5},{5,6},{6,7},{7,0},{8,9},{9,10},{10,1... | collective-permute-start | bytes 122888 | tf_op jit(solution)/shard_map/ppermute | solution.py:22
  56.3 4.6 %collective-permute-start.8 = (f32[5,8,2,128]{3,2,1,0:T(2,128)S(1)}, f32[5,8,2,128]{3,2,1,0:T(2,128)S(1)}, u32[]{:S(2)}, u32[]{:S(2)}) collective-permute-start(f32[5,8,2,128]{3,2,1,0:T(2,128)S(1)} %get-tuple-element.728), channel_id=1, source_target_pairs={{1,0},{2,1},{3,2},{4,3},{5,4},{6,5},{7,6},{0,7},{9,8},{10,9},{11,1... | collective-permute-start | bytes 122888 | tf_op jit(solution)/shard_map/ppermute | solution.py:23
  61.2 0.7 copy-start.3
  61.3 0.7 copy-start.8
  61.3 0.7 copy-start.9
  63.5 14.6 %collective-permute-start.10 = (f32[5,2,8,128]{3,2,1,0:T(8,128)S(1)}, f32[5,2,8,128]{3,2,1,0:T(8,128)S(1)}, u32[]{:S(2)}, u32[]{:S(2)}) collective-permute-start(f32[5,2,8,128]{3,2,1,0:T(8,128)S(1)} %get-tuple-element.721), channel_id=1, source_target_pairs={{0,8},{8,16},{16,24},{24,32},{32,40},{40,48},{48,56},{56,64},{64,7... | collective-permute-start | bytes 122888 | tf_op jit(solution)/shard_map/ppermute | solution.py:22
  65.5 13.2 %collective-permute-start.11 = (f32[5,2,8,128]{3,2,1,0:T(8,128)S(1)}, f32[5,2,8,128]{3,2,1,0:T(8,128)S(1)}, u32[]{:S(2)}, u32[]{:S(2)}) collective-permute-start(f32[5,2,8,128]{3,2,1,0:T(8,128)S(1)} %get-tuple-element.722), channel_id=1, source_target_pairs={{8,0},{16,8},{24,16},{32,24},{40,32},{48,40},{56,48},{64,56},{72,6... | collective-permute-start | bytes 122888 | tf_op jit(solution)/shard_map/ppermute | solution.py:23
  77.5 1.7 %collective-permute-start.9 = (f32[5,8,2,128]{3,2,1,0:T(2,128)S(1)}, f32[5,8,2,128]{3,2,1,0:T(2,128)S(1)}, u32[]{:S(2)}, u32[]{:S(2)}) collective-permute-start(f32[5,8,2,128]{3,2,1,0:T(2,128)S(1)} %get-tuple-element.723), channel_id=1, source_target_pairs={{0,1},{1,2},{2,3},{3,4},{4,5},{5,6},{6,7},{7,0},{8,9},{9,10},{10,1... | collective-permute-start | bytes 122888 | tf_op jit(solution)/shard_map/ppermute | solution.py:22
  78.1 4.6 %collective-permute-start.12 = (f32[5,8,2,128]{3,2,1,0:T(2,128)S(1)}, f32[5,8,2,128]{3,2,1,0:T(2,128)S(1)}, u32[]{:S(2)}, u32[]{:S(2)}) collective-permute-start(f32[5,8,2,128]{3,2,1,0:T(2,128)S(1)} %get-tuple-element.724), channel_id=1, source_target_pairs={{1,0},{2,1},{3,2},{4,3},{5,4},{6,5},{7,6},{0,7},{9,8},{10,9},{11,1... | collective-permute-start | bytes 122888 | tf_op jit(solution)/shard_map/ppermute | solution.py:23
  83.1 0.7 copy-start.4
  83.1 0.7 copy-start.10
  83.1 0.7 copy-start.11
  85.4 14.6 %collective-permute-start.14 = (f32[5,2,8,128]{3,2,1,0:T(8,128)S(1)}, f32[5,2,8,128]{3,2,1,0:T(8,128)S(1)}, u32[]{:S(2)}, u32[]{:S(2)}) collective-permute-start(f32[5,2,8,128]{3,2,1,0:T(8,128)S(1)} %get-tuple-element.717), channel_id=1, source_target_pairs={{0,8},{8,16},{16,24},{24,32},{32,40},{40,48},{48,56},{56,64},{64,7... | collective-permute-start | bytes 122888 | tf_op jit(solution)/shard_map/ppermute | solution.py:22
  87.3 13.2 %collective-permute-start.15 = (f32[5,2,8,128]{3,2,1,0:T(8,128)S(1)}, f32[5,2,8,128]{3,2,1,0:T(8,128)S(1)}, u32[]{:S(2)}, u32[]{:S(2)}) collective-permute-start(f32[5,2,8,128]{3,2,1,0:T(8,128)S(1)} %get-tuple-element.718), channel_id=1, source_target_pairs={{8,0},{16,8},{24,16},{32,24},{40,32},{48,40},{56,48},{64,56},{72,6... | collective-permute-start | bytes 122888 | tf_op jit(solution)/shard_map/ppermute | solution.py:23
  99.4 1.7 %collective-permute-start.13 = (f32[5,8,2,128]{3,2,1,0:T(2,128)S(1)}, f32[5,8,2,128]{3,2,1,0:T(2,128)S(1)}, u32[]{:S(2)}, u32[]{:S(2)}) collective-permute-start(f32[5,8,2,128]{3,2,1,0:T(2,128)S(1)} %get-tuple-element.719), channel_id=1, source_target_pairs={{0,1},{1,2},{2,3},{3,4},{4,5},{5,6},{6,7},{7,0},{8,9},{9,10},{10,1... | collective-permute-start | bytes 122888 | tf_op jit(solution)/shard_map/ppermute | solution.py:22
  99.9 4.6 %collective-permute-start.16 = (f32[5,8,2,128]{3,2,1,0:T(2,128)S(1)}, f32[5,8,2,128]{3,2,1,0:T(2,128)S(1)}, u32[]{:S(2)}, u32[]{:S(2)}) collective-permute-start(f32[5,8,2,128]{3,2,1,0:T(2,128)S(1)} %get-tuple-element.720), channel_id=1, source_target_pairs={{1,0},{2,1},{3,2},{4,3},{5,4},{6,5},{7,6},{0,7},{9,8},{10,9},{11,1... | collective-permute-start | bytes 122888 | tf_op jit(solution)/shard_map/ppermute | solution.py:23
  104.9 0.7 copy-start.5
  104.9 0.7 copy-start.12
  104.9 0.7 copy-start.13
where the time goes:
time: 108 us
  starting transfers between devices  74.5 us (69%)
  waiting for transfers between devices  19.7 us (18%)
  local copies, waits for them, and re-layouts  7.22 us (7%)
  other arithmetic  5.48 us (5%)
    ppermute x8, starting transfers between devices, extended(): lax.ppermute(leading, axis, [(b, a) for a, b in up])  50.1 us
    ppermute x8, waiting for transfers between devices, extended(): lax.ppermute(leading, axis, [(b, a) for a, b in up])  15.1 us
    ppermute x8, starting transfers between devices, extended(): lax.ppermute(last, axis, up)  15 us
    ppermute x1, starting transfers between devices, from_behind(): lax.ppermute(value, axis, [(source, source + steps) for source in range(l...  9.4 us
    slice x20, local copies, waits for them, and re-layouts, offset_cells(): jnp.roll(values[..., 2:length_x - 2, 2:length_y - 2, :], -shift_by, axis=-1)  2.85 us
    cond x24, local copies, waits for them, and re-layouts  2.66 us
    ppermute x8, waiting for transfers between devices, extended(): lax.ppermute(last, axis, up)  2.54 us
    add x4, other arithmetic, flow_rate(): return total + VISCOSITY * spread  2.25 us
  transfers between devices with their start and end apart: 17, of which 11 were waited for; matrix products, arithmetic and copies ran while one was open for 0% of the time, Pallas kernels for 0%

commit v1 on v0

v1 whole, which is shorter than its diff:
```python
import functools

import jax
import jax.numpy as jnp
from jax import lax
from jax.experimental import pallas as pl
from jax.experimental.pallas import tpu as pltpu
from jax.sharding import PartitionSpec as P

MESH = pl.DeviceIdType.MESH
MBLEN = 4
GAMMA = 1.4
STEP_DT = 0.2
VISCOSITY = 0.05

EX = 8
EY = 8
HY = 4
WX = 3 * EX
WY = EY + 2 * HY

DIRECTIONS = ((1, 0), (-1, 0), (1, 1), (1, -1), (-1, 1), (-1, -1), (0, 1), (0, -1))

FIELD, MEAN, SPEED, PARTNER, STAGE = 0, 8, 16, 24, 25
SEMAPHORES = 27


def whole_x(dx):
    source = pl.ds(0, EX)
    target = pl.ds({1: 0, 0: EX, -1: 2 * EX}[dx], EX)
    return source, target


def part_x(dx, width):
    source = pl.ds({1: EX - width, 0: 0, -1: 0}[dx], EX if dx == 0 else width)
    target = pl.ds({1: EX - width, 0: EX, -1: 2 * EX}[dx], EX if dx == 0 else width)
    return source, target


def part_y(dy, width):
    source = ({1: EY - width, 0: 0, -1: 0}[dy], EY if dy == 0 else width)
    target = ({1: HY - width, 0: HY, -1: HY + EY}[dy], EY if dy == 0 else width)
    return source, target


def shift(values, axis, by):
    size = values.shape[axis]
    return pltpu.roll(values, (-by) % size, axis)


def derivative(values, axis):
    once = shift(values, axis, 1) - shift(values, axis, -1)
    return 8.0 * once - (shift(once, axis, 1) + shift(once, axis, -1))


def derivative_x(ref, c, x):
    return 8.0 * (ref[c, x + 1] - ref[c, x - 1]) - (ref[c, x + 2] - ref[c, x - 2])


def primitives(q):
    inverse = 1.0 / q[0]
    u = [q[1 + j] * inverse for j in range(3)]
    p = (GAMMA - 1.0) * (q[4] - 0.5 * (q[1] * u[0] + q[2] * u[1] + q[3] * u[2]))
    return u, p


def flux(q, u, p, d):
    parts = [q[1 + d]]
    for j in range(3):
        part = q[1 + j] * u[d]
        parts.append(part + p if j == d else part)
    parts.append((q[4] + p) * u[d])
    return parts


def fluxes_x(q_ref, f_ref, low, high):
    def row(x, carry):
        q = [q_ref[c, x] for c in range(5)]
        u, p = primitives(q)
        f = flux(q, u, p, 0)
        for c in range(1, 5):
            f_ref[c - 1, x] = f[c]
        return carry

    lax.fori_loop(low, high, row, 0)


def flow_row(q_ref, f_ref, x):
    q = [q_ref[c, x] for c in range(5)]
    u, p = primitives(q)
    along_y = flux(q, u, p, 1)
    along_z = flux(q, u, p, 2)
    rates = []
    for c in range(5):
        f, fc = (q_ref, 1) if c == 0 else (f_ref, c - 1)
        total = 8.0 * (f[fc, x - 1] - f[fc, x + 1]) + (f[fc, x + 2] - f[fc, x - 2])
        total += (16.0 * VISCOSITY) * (q_ref[c, x + 1] + q_ref[c, x - 1])
        total -= VISCOSITY * (q_ref[c, x + 2] + q_ref[c, x - 2])
        total -= (90.0 * VISCOSITY) * q[c]
        near, far = ((16.0 * VISCOSITY) * q[c], VISCOSITY * q[c])
        for axis, parts in ((0, along_y), (1, along_z)):
            eight = 8.0 * parts[c]
            total += shift(near - eight, axis, 1) + shift(near + eight, axis, -1)
            total += shift(parts[c] - far, axis, 2) - shift(parts[c] + far, axis, -2)
        rates.append(total * (1.0 / 12.0))
    return rates


def sound_row(a_ref, mean_ref, x):
    mean = [mean_ref[c, x] for c in range(5)]
    speed = [mean[j] * (1.0 / 12.0) for j in range(3)]
    density = mean[3] * (1.0 / 12.0)
    inverse = (1.0 / 12.0) / mean[3]
    slopes, carried = [], []
    for c in range(5):
        value = a_ref[c, x]
        d = [derivative_x(a_ref, c, x), derivative(value, 0), derivative(value, 1)]
        slopes.append(d)
        carried.append(speed[0] * d[0] + speed[1] * d[1] + speed[2] * d[2])
    divergence = density * (slopes[1][0] + slopes[2][1] + slopes[3][2])
    rates = [-carried[0] - divergence]
    for j in range(3):
        rates.append(-carried[1 + j] - slopes[4][j] * inverse)
    rates.append(-carried[4] - mean[4] * mean[4] * divergence)
    return rates


def lamb_row(u_ref, x):
    u = [u_ref[c, x] for c in range(3)]
    spin = (
        derivative(u[2], 0) - derivative(u[1], 1),
        derivative(u[0], 1) - derivative_x(u_ref, 2, x),
        derivative_x(u_ref, 1, x) - derivative(u[0], 0),
    )
    scale = 1.0 / 12.0
    return [
        scale * (spin[1] * u[2] - spin[2] * u[1]),
        scale * (spin[2] * u[0] - spin[0] * u[2]),
        scale * (spin[0] * u[1] - spin[1] * u[0]),
    ]


def kernel(
    nx,
    nr,
    fields,
    mean_flow,
    blocks,
    out,
    own,
    own_mean,
    own_speed,
    start,
    mean,
    speed,
    source,
    odd,
    even,
    flux_x,
    slope,
    send,
    receive,
    local,
):
    sec = lax.axis_index("sec")
    gx = lax.axis_index("gx")
    row = lax.axis_index("row")
    is_flow = sec == 0
    is_sound = sec == 1
    first, last = gx == 0, gx == nx - 1

    def place(section, dx, dy):
        return {
            "sec": section,
            "gx": lax.rem(gx + dx + nx, nx),
            "row": lax.rem(row + dy + nr, nr),
        }

    barrier = pltpu.get_barrier_semaphore()

    def greet(device):
        pl.semaphore_signal(barrier, inc=1, device_id=device, device_id_type=MESH)

    greet(place(1 - sec, 0, 0))
    for dx, dy in DIRECTIONS:
        greet(place(sec, dx, dy))
    for edge, dx in ((first, -1), (last, 1)):

        @pl.when(edge)
        def _():
            for dy in (-1, 0, 1):
                greet(place(1 - sec, dx, dy))

    inner_x, inner_y = pl.ds(EX, EX), pl.ds(HY, EY)
    load = pltpu.make_async_copy(fields.at[0], own, local.at[0])
    load.start()
    load_start = pltpu.make_async_copy(fields.at[0], start.at[:, inner_x, inner_y], local.at[1])
    load_start.start()
    load_mean = pltpu.make_async_copy(mean_flow, own_mean, local.at[2])
    load_inner = pltpu.make_async_copy(mean_flow, mean.at[:, inner_x, inner_y], local.at[3])

    @pl.when(is_sound)
    def _():
        load_mean.start()
        load_inner.start()

    load.wait()

    @pl.when(is_flow)
    def _():
        for x in range(EX):
            inverse = 1.0 / own[0, x]
            for j in range(3):
                own_speed[j, x] = own[1 + j, x] * inverse

    @pl.when(is_sound)
    def _():
        load_mean.wait()

    @pl.when(first | last)
    def _():
        pl.semaphore_wait(barrier, 12)

    @pl.when((gx > 0) & (gx < nx - 1))
    def _():
        pl.semaphore_wait(barrier, 9)

    def remote(origin, target, index, device):
        return pltpu.make_async_remote_copy(
            src_ref=origin,
            dst_ref=target,
            send_sem=send.at[index],
            recv_sem=receive.at[index],
            device_id=device,
            device_id_type=MESH,
        )

    def field_copy(i):
        dx, dy = DIRECTIONS[i]
        (sx, tx), (sy, ty) = whole_x(dx), part_y(dy, HY)
        return remote(
            own.at[:, sx, pl.ds(*sy)], start.at[:, tx, pl.ds(*ty)], FIELD + i, place(sec, dx, dy)
        )

    def mean_copy(i):
        dx, dy = DIRECTIONS[i]
        (sx, tx), (sy, ty) = part_x(dx, EX - 2), part_y(dy, HY - 2)
        return remote(
            own_mean.at[:, sx, pl.ds(*sy)], mean.at[:, tx, pl.ds(*ty)], MEAN + i, place(sec, dx, dy)
        )

    def speed_copy(i):
        dx, dy = DIRECTIONS[i]
        (_, tx), (sy, ty) = whole_x(dx), part_y(dy, HY)
        return remote(
            speed.at[:, inner_x, pl.ds(HY + sy[0], sy[1])],
            speed.at[:, tx, pl.ds(*ty)],
            SPEED + i,
            place(1, dx, dy),
        )

    def speed_around(i):
        dx, dy = DIRECTIONS[i]
        (sx, tx), (sy, ty) = whole_x(dx), part_y(dy, HY)
        return remote(
            own_speed.at[:, sx, pl.ds(*sy)],
            speed.at[:, tx, pl.ds(*ty)],
            SPEED + i,
            place(1, dx, dy),
        )

    partner_copy = remote(own_speed, speed.at[:, inner_x, inner_y], PARTNER, place(1, 0, 0))
    up = [i for i, d in enumerate(DIRECTIONS) if d[0] == 1]
    down = [i for i, d in enumerate(DIRECTIONS) if d[0] == -1]
    level = [i for i, d in enumerate(DIRECTIONS) if d[0] == 0]
    every = range(len(DIRECTIONS))

    @pl.when(is_flow)
    def _():
        partner_copy.start()

    for i in every:
        field_copy(i).start()

    @pl.when(is_flow & last)
    def _():
        for i in up:
            speed_around(i).start()

    @pl.when(is_flow & first)
    def _():
        for i in down:
            speed_around(i).start()

    @pl.when(is_sound)
    def _():
        for i in every:
            mean_copy(i).start()

    def stage_copies(ref):
        rows = pl.ds(4, WX - 8)
        return [
            remote(
                ref.at[:, rows, pl.ds(HY + EY - HY, HY)],
                ref.at[:, rows, pl.ds(0, HY)],
                STAGE,
                place(sec, 0, 1),
            ),
            remote(
                ref.at[:, rows, pl.ds(HY, HY)],
                ref.at[:, rows, pl.ds(HY + EY, HY)],
                STAGE + 1,
                place(sec, 0, -1),
            ),
        ]

    def advance(rate, prepare):
        prepare(odd, 2, WX - 2)

        def second(x, carry):
            for c, k in enumerate(rate(odd, x)):
                state = start[c, x] + (0.5 * STEP_DT) * k
                even[c, x, HY : HY + EY] = state[HY : HY + EY]
                slope[c, x] += 2.0 * k
            return carry

        lax.fori_loop(4, WX - 4, second, 0)
        copies = stage_copies(even)
        for copy in copies:
            copy.start()
        for copy in copies:
            copy.wait()
        prepare(even, 4, WX - 4)

        def third(x, carry):
            for c, k in enumerate(rate(even, x)):
                odd[c, x] = start[c, x] + STEP_DT * k
                slope[c, x] += 2.0 * k
            return carry

        lax.fori_loop(6, WX - 6, third, 0)
        prepare(odd, 6, WX - 6)

        def fourth(x, carry):
            for c, k in enumerate(rate(odd, x)):
                state = start[c, x] + (STEP_DT / 6.0) * (slope[c, x] + k)
                out[0, c, x - EX] = state[HY : HY + EY]
            return carry

        lax.fori_loop(EX, 2 * EX, fourth, 0)

    load_start.wait()

    @pl.when(is_flow)
    def _():
        for i in every:
            field_copy(i).wait_recv()

        def rate(ref, x):
            return flow_row(ref, flux_x, x)

        def prepare(ref, low, high):
            fluxes_x(ref, flux_x, low, high)

        prepare(start, 0, WX)

        def one(x, carry):
            for c, k in enumerate(rate(start, x)):
                odd[c, x] = start[c, x] + (0.5 * STEP_DT) * k
                slope[c, x] = k
            return carry

        lax.fori_loop(2, WX - 2, one, 0)
        advance(rate, prepare)
        partner_copy.wait_send()

    @pl.when(is_sound)
    def _():
        partner_copy.wait_recv()
        for i in level:
            speed_copy(i).start()

        @pl.when(gx < nx - 1)
        def _():
            for i in up:
                speed_copy(i).start()

        @pl.when(gx > 0)
        def _():
            for i in down:
                speed_copy(i).start()

        for i in every:
            field_copy(i).wait_recv()
            mean_copy(i).wait_recv()
        load_inner.wait()

        def plain(x, carry):
            for c, k in enumerate(sound_row(start, mean, x)):
                slope[c, x] = k
            return carry

        lax.fori_loop(2, WX - 2, plain, 0)
        for i in every:
            speed_copy(i).wait_recv()

        cells = nx * EX

        def one(x, carry):
            block = lax.rem(gx * EX + x - EX + cells, cells) // MBLEN
            mask = blocks[block].astype(jnp.float32)
            terms = [mask * part for part in lamb_row(speed, x)]
            for c in range(5):
                k = slope[c, x]
                if 1 <= c <= 3:
                    source[c - 1, x] = terms[c - 1]
                    k = k - terms[c - 1]
                    slope[c, x] = k
                odd[c, x] = start[c, x] + (0.5 * STEP_DT) * k
            return carry

        lax.fori_loop(2, WX - 2, one, 0)

        def rate(ref, x):
            rates = sound_row(ref, mean, x)
            return [
                k - source[c - 1, x] if 1 <= c <= 3 else k for c, k in enumerate(rates)
            ]

        advance(rate, lambda ref, low, high: None)
        for i in level:
            speed_copy(i).wait_send()

        @pl.when(gx < nx - 1)
        def _():
            for i in up:
                speed_copy(i).wait_send()

        @pl.when(gx > 0)
        def _():
            for i in down:
                speed_copy(i).wait_send()

        for i in every:
            mean_copy(i).wait_send()

    for i in every:
        field_copy(i).wait_send()

    @pl.when(is_flow & last)
    def _():
        for i in up:
            speed_around(i).wait_send()

    @pl.when(is_flow & first)
    def _():
        for i in down:
            speed_around(i).wait_send()


def solution(mesh):
    nx, nr = mesh.shape["gx"], mesh.shape["row"]

    def local(fields, mean_flow, source_blocks):
        window = (WX, WY, 128)
        return pl.pallas_call(
            functools.partial(kernel, nx, nr),
            out_shape=jax.ShapeDtypeStruct(fields.shape, jnp.float32),
            in_specs=[
                pl.BlockSpec(memory_space=pl.ANY),
                pl.BlockSpec(memory_space=pl.ANY),
                pl.BlockSpec(memory_space=pltpu.SMEM),
            ],
            out_specs=pl.BlockSpec(memory_space=pltpu.VMEM),
            scratch_shapes=[
                pltpu.VMEM((5, EX, EY, 128), jnp.float32),
                pltpu.VMEM((5, EX, EY, 128), jnp.float32),
                pltpu.VMEM((3, EX, EY, 128), jnp.float32),
                pltpu.VMEM((5,) + window, jnp.float32),
                pltpu.VMEM((5,) + window, jnp.float32),
                pltpu.VMEM((3,) + window, jnp.float32),
                pltpu.VMEM((3,) + window, jnp.float32),
                pltpu.VMEM((5,) + window, jnp.float32),
                pltpu.VMEM((5,) + window, jnp.float32),
                pltpu.VMEM((4,) + window, jnp.float32),
                pltpu.VMEM((5,) + window, jnp.float32),
                pltpu.SemaphoreType.DMA((SEMAPHORES,)),
                pltpu.SemaphoreType.DMA((SEMAPHORES,)),
                pltpu.SemaphoreType.DMA((4,)),
            ],
            compiler_params=pltpu.CompilerParams(collective_id=0, has_side_effects=True),
        )(fields, mean_flow, source_blocks)

    return jax.shard_map(
        local,
        mesh=mesh,
        in_specs=(P("sec", None, "gx", "row", None), P(None, "gx", "row", None), P()),
        out_specs=P("sec", None, "gx", "row", None),
        check_vma=False,
    )
```

time: 108 us -> 54.2 us (0.50)
  the two profiles are of different devices: /device:TPU:25 before, /device:TPU:320 now
where the time goes in v1:
time: 54.2 us; the launch traced here: 54.1 us
  Pallas kernels  52.5 us (97%)
  local copies, waits for them, and re-layouts  1.59 us (3%)
    pallas_call x1, Pallas kernels, local(): pl.pallas_call(functools.partial(kernel, nx, nr), out_shape=jax.ShapeDtyp...  52.5 us
    unnamed x1, local copies, waits for them, and re-layouts  1.59 us

profile of v1, /device:TPU:320, one launch (start us, length us, event | category | flops | bytes accessed | tf_op | source)
XLA Modules:
  0.0 54.1 jit_solution(12272088495135028951)
XLA Ops:
  0.0 52.5 %shard_map.37 = f32[1,5,8,8,128]{4,3,2,1,0:T(8,128)} custom-call(f32[1,5,8,8,128]{4,3,2,1,0:T(8,128)} %fields.1, f32[5,8,8,128]{3,2,1,0:T(8,128)} %mean_flow.1, s32[64]{0:T(128)} %blocks.1), custom_call_target="tpu_custom_call" | custom-call | tf_op jit(solution)/shard_map/pallas_call | solution.py:466
  52.5 1.6 %copy.5 = f32[1,5,8,8,128]{4,3,2,1,0:T(8,128)} copy(f32[1,5,8,8,128]{4,3,2,1,0:T(8,128)} %shard_map.37) | data formatting | bytes 327680

commit v2 on v1

v2 whole, which is shorter than its diff:
```python
import functools

import jax
import jax.numpy as jnp
from jax import lax
from jax.experimental import pallas as pl
from jax.experimental.pallas import tpu as pltpu
from jax.sharding import PartitionSpec as P

MESH = pl.DeviceIdType.MESH
MBLEN = 4
GAMMA = 1.4
STEP_DT = 0.2
VISCOSITY = 0.05

OWN = 8
HALO = 4
WIDE = OWN + 2 * HALO

DIRECTIONS = ((1, 0), (-1, 0), (0, 1), (0, -1), (1, 1), (1, -1), (-1, 1), (-1, -1))

FIELD, SPEED, STAGE, MEAN, PARTNER = 0, 8, 16, 24, 32
SEMAPHORES = 33


def part(d, width):
    if d == 1:
        return OWN - width, HALO - width, width
    if d == -1:
        return 0, HALO + OWN, width
    return 0, HALO, OWN


def parts(direction, width):
    if direction[0] and direction[1]:
        width = 2
    (sx, tx, nx), (sy, ty, ny) = part(direction[0], width), part(direction[1], width)
    return (
        (slice(None), pl.ds(sx, nx), pl.ds(sy, ny)),
        (slice(None), pl.ds(HALO + sx, nx), pl.ds(HALO + sy, ny)),
        (slice(None), pl.ds(tx, nx), pl.ds(ty, ny)),
    )


def shift(values, axis, by):
    size = values.shape[axis]
    return pltpu.roll(values, (-by) % size, axis)


def derivative(values, axis):
    once = shift(values, axis, 1) - shift(values, axis, -1)
    return 8.0 * once - (shift(once, axis, 1) + shift(once, axis, -1))


def derivative_x(ref, c, x):
    return 8.0 * (ref[c, x + 1] - ref[c, x - 1]) - (ref[c, x + 2] - ref[c, x - 2])


def primitives(q):
    inverse = 1.0 / q[0]
    u = [q[1 + j] * inverse for j in range(3)]
    p = (GAMMA - 1.0) * (q[4] - 0.5 * (q[1] * u[0] + q[2] * u[1] + q[3] * u[2]))
    return u, p


def flux(q, u, p, d):
    parts = [q[1 + d]]
    for j in range(3):
        part = q[1 + j] * u[d]
        parts.append(part + p if j == d else part)
    parts.append((q[4] + p) * u[d])
    return parts


def fluxes_x(q_ref, f_ref, low, high):
    def row(x, carry):
        q = [q_ref[c, x] for c in range(5)]
        u, p = primitives(q)
        f = flux(q, u, p, 0)
        for c in range(1, 5):
            f_ref[c - 1, x] = f[c]
        return carry

    lax.fori_loop(low, high, row, 0)


def flow_row(q_ref, f_ref, x):
    q = [q_ref[c, x] for c in range(5)]
    u, p = primitives(q)
    along_y = flux(q, u, p, 1)
    along_z = flux(q, u, p, 2)
    rates = []
    for c in range(5):
        f, fc = (q_ref, 1) if c == 0 else (f_ref, c - 1)
        total = 8.0 * (f[fc, x - 1] - f[fc, x + 1]) + (f[fc, x + 2] - f[fc, x - 2])
        total += (16.0 * VISCOSITY) * (q_ref[c, x + 1] + q_ref[c, x - 1])
        total -= VISCOSITY * (q_ref[c, x + 2] + q_ref[c, x - 2])
        total -= (90.0 * VISCOSITY) * q[c]
        near, far = ((16.0 * VISCOSITY) * q[c], VISCOSITY * q[c])
        for axis, parts in ((0, along_y), (1, along_z)):
            eight = 8.0 * parts[c]
            total += shift(near - eight, axis, 1) + shift(near + eight, axis, -1)
            total += shift(parts[c] - far, axis, 2) - shift(parts[c] + far, axis, -2)
        rates.append(total * (1.0 / 12.0))
    return rates


def sound_row(a_ref, mean_ref, x):
    mean = [mean_ref[c, x] for c in range(5)]
    speed = [mean[j] * (1.0 / 12.0) for j in range(3)]
    density = mean[3] * (1.0 / 12.0)
    inverse = (1.0 / 12.0) / mean[3]
    slopes, carried = [], []
    for c in range(5):
        value = a_ref[c, x]
        d = [derivative_x(a_ref, c, x), derivative(value, 0), derivative(value, 1)]
        slopes.append(d)
        carried.append(speed[0] * d[0] + speed[1] * d[1] + speed[2] * d[2])
    divergence = density * (slopes[1][0] + slopes[2][1] + slopes[3][2])
    rates = [-carried[0] - divergence]
    for j in range(3):
        rates.append(-carried[1 + j] - slopes[4][j] * inverse)
    rates.append(-carried[4] - mean[4] * mean[4] * divergence)
    return rates


def lamb_row(u_ref, x):
    u = [u_ref[c, x] for c in range(3)]
    spin = (
        derivative(u[2], 0) - derivative(u[1], 1),
        derivative(u[0], 1) - derivative_x(u_ref, 2, x),
        derivative_x(u_ref, 1, x) - derivative(u[0], 0),
    )
    scale = 1.0 / 12.0
    return [
        scale * (spin[1] * u[2] - spin[2] * u[1]),
        scale * (spin[2] * u[0] - spin[0] * u[2]),
        scale * (spin[0] * u[1] - spin[1] * u[0]),
    ]


def kernel(
    nx,
    nr,
    fields,
    mean_flow,
    blocks,
    out,
    own,
    own_mean,
    own_speed,
    start,
    mean,
    speed,
    source,
    odd,
    even,
    flux_x,
    slope,
    send,
    receive,
    local,
    ready,
):
    sec = lax.axis_index("sec")
    gx = lax.axis_index("gx")
    row = lax.axis_index("row")
    is_flow = sec == 0
    is_sound = sec == 1
    first, last = gx == 0, gx == nx - 1

    def place(section, dx, dy):
        return {
            "sec": section,
            "gx": lax.rem(gx + dx + nx, nx),
            "row": lax.rem(row + dy + nr, nr),
        }

    barrier = pltpu.get_barrier_semaphore()

    def greet(device):
        pl.semaphore_signal(barrier, inc=1, device_id=device, device_id_type=MESH)

    for dx, dy in DIRECTIONS:
        greet(place(sec, dx, dy))

    @pl.when((is_sound & (gx < nx - 1)) | (is_flow & last))
    def _():
        greet(place(1 - sec, 0, 0))

    @pl.when(is_sound & first)
    def _():
        for dy in (-1, 0, 1):
            greet(place(0, -1, dy))

    @pl.when(is_sound & last)
    def _():
        for dy in (-1, 0, 1):
            greet(place(0, 1, dy))

    inner = (slice(None), pl.ds(HALO, OWN), pl.ds(HALO, OWN))
    load = pltpu.make_async_copy(fields.at[0], own, local.at[0])
    load.start()
    load_start = pltpu.make_async_copy(fields.at[0], start.at[inner], local.at[1])
    load_start.start()
    load_mean = pltpu.make_async_copy(mean_flow, own_mean, local.at[2])
    load_inner = pltpu.make_async_copy(mean_flow, mean.at[inner], local.at[3])

    @pl.when(is_sound)
    def _():
        load_mean.start()
        load_inner.start()

    load.wait()

    @pl.when(is_flow)
    def _():
        for x in range(OWN):
            inverse = 1.0 / own[0, x]
            for j in range(3):
                own_speed[j, x] = own[1 + j, x] * inverse

    @pl.when(is_sound)
    def _():
        load_mean.wait()

    for found, peers in (
        (is_flow & first, 12),
        (is_flow & (gx > 0) & (gx < nx - 1), 9),
        (is_flow & last, 11),
        (is_sound & (gx < nx - 1), 8),
        (is_sound & last, 9),
    ):

        @pl.when(found)
        def _():
            pl.semaphore_wait(barrier, peers)

    @pl.when(is_sound & last)
    def _():
        pl.semaphore_signal(ready, inc=1, device_id=place(0, 0, 0), device_id_type=MESH)

    def remote(origin, target, index, device):
        return pltpu.make_async_remote_copy(
            src_ref=origin,
            dst_ref=target,
            send_sem=send.at[index],
            recv_sem=receive.at[index],
            device_id=device,
            device_id_type=MESH,
        )

    def copies(section, origin, held, target, base, count=8, width=HALO):
        made = []
        for i in range(count):
            block, middle, slot = parts(DIRECTIONS[i], width)
            made.append(
                remote(
                    origin.at[middle if held else block],
                    target.at[slot],
                    base + i,
                    place(section, *DIRECTIONS[i]),
                )
            )
        return made

    field_copies = copies(sec, own, False, start, FIELD)
    mean_copies = copies(1, own_mean, False, mean, MEAN, count=4, width=2)
    speed_copies = copies(1, speed, True, speed, SPEED)
    around = copies(1, own_speed, False, speed, SPEED)
    stage_copies = copies(sec, even, True, even, STAGE)
    partner_copy = remote(own_speed, speed.at[inner], PARTNER, place(1, 0, 0))
    up = [i for i, d in enumerate(DIRECTIONS) if d[0] == 1]
    down = [i for i, d in enumerate(DIRECTIONS) if d[0] == -1]
    level = [i for i, d in enumerate(DIRECTIONS) if d[0] == 0]

    @pl.when(is_flow & (gx < nx - 1))
    def _():
        partner_copy.start()

    for copy in field_copies:
        copy.start()

    @pl.when(is_flow & first)
    def _():
        for i in down:
            around[i].start()

    @pl.when(is_flow & last)
    def _():
        for i in up:
            around[i].start()
        pl.semaphore_wait(ready, 1)
        partner_copy.start()

    @pl.when(is_sound)
    def _():
        for copy in mean_copies:
            copy.start()

    def advance(rate, prepare):
        prepare(odd, 2, WIDE - 2)

        def second(x, carry):
            for c, k in enumerate(rate(odd, x)):
                state = start[c, x] + (0.5 * STEP_DT) * k
                even[c, x, HALO : HALO + OWN] = state[HALO : HALO + OWN]
                slope[c, x] += 2.0 * k
            return carry

        lax.fori_loop(HALO, HALO + OWN, second, 0)
        for copy in stage_copies:
            copy.start()
        for copy in stage_copies:
            copy.wait()
        prepare(even, 0, WIDE)

        def third(x, carry):
            for c, k in enumerate(rate(even, x)):
                odd[c, x] = start[c, x] + STEP_DT * k
                slope[c, x] += 2.0 * k
            return carry

        lax.fori_loop(2, WIDE - 2, third, 0)
        prepare(odd, 2, WIDE - 2)

        def fourth(x, carry):
            for c, k in enumerate(rate(odd, x)):
                state = start[c, x] + (STEP_DT / 6.0) * (slope[c, x] + k)
                out[0, c, x - HALO] = state[HALO : HALO + OWN]
            return carry

        lax.fori_loop(HALO, HALO + OWN, fourth, 0)

    load_start.wait()

    @pl.when(is_flow)
    def _():
        for copy in field_copies:
            copy.wait_recv()

        def rate(ref, x):
            return flow_row(ref, flux_x, x)

        def prepare(ref, low, high):
            fluxes_x(ref, flux_x, low, high)

        prepare(start, 0, WIDE)

        def one(x, carry):
            for c, k in enumerate(rate(start, x)):
                odd[c, x] = start[c, x] + (0.5 * STEP_DT) * k
                slope[c, x] = k
            return carry

        lax.fori_loop(2, WIDE - 2, one, 0)

        advance(rate, prepare)
        partner_copy.wait_send()

    @pl.when(is_sound)
    def _():
        partner_copy.wait_recv()
        for i in level:
            speed_copies[i].start()

        @pl.when(gx < nx - 1)
        def _():
            for i in up:
                speed_copies[i].start()

        @pl.when(gx > 0)
        def _():
            for i in down:
                speed_copies[i].start()

        for copy in field_copies + mean_copies:
            copy.wait_recv()
        load_inner.wait()

        def plain(x, carry):
            for c, k in enumerate(sound_row(start, mean, x)):
                slope[c, x] = k
            return carry

        lax.fori_loop(2, WIDE - 2, plain, 0)
        for copy in speed_copies:
            copy.wait_recv()

        cells = nx * OWN

        def one(x, carry):
            block = lax.rem(gx * OWN + x - HALO + cells, cells) // MBLEN
            mask = blocks[block].astype(jnp.float32)
            terms = [mask * part for part in lamb_row(speed, x)]
            for c in range(5):
                k = slope[c, x]
                if 1 <= c <= 3:
                    source[c - 1, x] = terms[c - 1]
                    k = k - terms[c - 1]
                    slope[c, x] = k
                odd[c, x] = start[c, x] + (0.5 * STEP_DT) * k
            return carry

        lax.fori_loop(2, WIDE - 2, one, 0)

        def rate(ref, x):
            rates = sound_row(ref, mean, x)
            return [
                k - source[c - 1, x] if 1 <= c <= 3 else k for c, k in enumerate(rates)
            ]

        advance(rate, lambda ref, low, high: None)
        for i in level:
            speed_copies[i].wait_send()

        @pl.when(gx < nx - 1)
        def _():
            for i in up:
                speed_copies[i].wait_send()

        @pl.when(gx > 0)
        def _():
            for i in down:
                speed_copies[i].wait_send()

        for copy in mean_copies:
            copy.wait_send()

    for copy in field_copies:
        copy.wait_send()

    @pl.when(is_flow & last)
    def _():
        for i in up:
            around[i].wait_send()

    @pl.when(is_flow & first)
    def _():
        for i in down:
            around[i].wait_send()


def solution(mesh):
    nx, nr = mesh.shape["gx"], mesh.shape["row"]

    def local(fields, mean_flow, source_blocks):
        window = (WIDE, WIDE, 128)
        return pl.pallas_call(
            functools.partial(kernel, nx, nr),
            out_shape=jax.ShapeDtypeStruct(fields.shape, jnp.float32),
            in_specs=[
                pl.BlockSpec(memory_space=pl.ANY),
                pl.BlockSpec(memory_space=pl.ANY),
                pl.BlockSpec(memory_space=pltpu.SMEM),
            ],
            out_specs=pl.BlockSpec(memory_space=pltpu.VMEM),
            scratch_shapes=[
                pltpu.VMEM((5, OWN, OWN, 128), jnp.float32),
                pltpu.VMEM((5, OWN, OWN, 128), jnp.float32),
                pltpu.VMEM((3, OWN, OWN, 128), jnp.float32),
                pltpu.VMEM((5,) + window, jnp.float32),
                pltpu.VMEM((5,) + window, jnp.float32),
                pltpu.VMEM((3,) + window, jnp.float32),
                pltpu.VMEM((3,) + window, jnp.float32),
                pltpu.VMEM((5,) + window, jnp.float32),
                pltpu.VMEM((5,) + window, jnp.float32),
                pltpu.VMEM((4,) + window, jnp.float32),
                pltpu.VMEM((5,) + window, jnp.float32),
                pltpu.SemaphoreType.DMA((SEMAPHORES,)),
                pltpu.SemaphoreType.DMA((SEMAPHORES,)),
                pltpu.SemaphoreType.DMA((4,)),
                pltpu.SemaphoreType.REGULAR,
            ],
            compiler_params=pltpu.CompilerParams(collective_id=0, has_side_effects=True),
        )(fields, mean_flow, source_blocks)

    return jax.shard_map(
        local,
        mesh=mesh,
        in_specs=(P("sec", None, "gx", "row", None), P(None, "gx", "row", None), P()),
        out_specs=P("sec", None, "gx", "row", None),
        check_vma=False,
    )
```

time: 54.2 us -> 46.5 us (0.86)
  the two profiles are of different devices: /device:TPU:320 before, /device:TPU:1 now
where the time goes in v2:
time: 46.5 us; the launch traced here: 46.3 us
  Pallas kernels  44.7 us (96%)
  local copies, waits for them, and re-layouts  1.59 us (3%)
    pallas_call x1, Pallas kernels, local(): pl.pallas_call(functools.partial(kernel, nx, nr), out_shape=jax.ShapeDtyp...  44.7 us
    unnamed x1, local copies, waits for them, and re-layouts  1.59 us

profile of v2, /device:TPU:1, one launch (start us, length us, event | category | flops | bytes accessed | tf_op | source)
XLA Modules:
  0.0 46.3 jit_solution(11785598284034758026)
XLA Ops:
  0.0 44.7 %shard_map.37 = f32[1,5,8,8,128]{4,3,2,1,0:T(8,128)} custom-call(f32[1,5,8,8,128]{4,3,2,1,0:T(8,128)} %fields.1, f32[5,8,8,128]{3,2,1,0:T(8,128)} %mean_flow.1, s32[64]{0:T(128)} %blocks.1), custom_call_target="tpu_custom_call" | custom-call | tf_op jit(solution)/shard_map/pallas_call | solution.py:449
  44.7 1.6 %copy.5 = f32[1,5,8,8,128]{4,3,2,1,0:T(8,128)} copy(f32[1,5,8,8,128]{4,3,2,1,0:T(8,128)} %shard_map.37) | data formatting | bytes 327680

commit v3 on v2

v3 whole, which is shorter than its diff:
```python
import functools

import jax
import jax.numpy as jnp
from jax import lax
from jax.experimental import pallas as pl
from jax.experimental.pallas import tpu as pltpu
from jax.sharding import PartitionSpec as P

MESH = pl.DeviceIdType.MESH
MBLEN = 4
GAMMA = 1.4
STEP_DT = 0.2
VISCOSITY = 0.05

OWN = 8
HALO = 4
BEGIN = (HALO, 8)
WINDOW = (OWN + 2 * HALO, 24, 128)

DIRECTIONS = ((1, 0), (-1, 0), (0, 1), (0, -1), (1, 1), (1, -1), (-1, 1), (-1, -1))

FIELD, SPEED, STAGE, MEAN, PARTNER = 0, 8, 16, 24, 32
SEMAPHORES = 33


def part(d, width, begin):
    if d == 1:
        return OWN - width, begin - width, width
    if d == -1:
        return 0, begin + OWN, width
    return 0, begin, OWN


def parts(direction, width):
    if direction[0] and direction[1]:
        width = 2
    both = [part(d, width, begin) for d, begin in zip(direction, BEGIN)]
    every = (slice(None),)
    return (
        every + tuple(pl.ds(s, n) for s, _, n in both),
        every + tuple(pl.ds(begin + s, n) for (s, _, n), begin in zip(both, BEGIN)),
        every + tuple(pl.ds(t, n) for _, t, n in both),
    )


def turn(values, by):
    return pltpu.roll(values, (-by) % values.shape[-1], values.ndim - 1)


class Block:
    def __init__(self, x, columns, y, rows):
        self.x, self.columns, self.y, self.rows = x, columns, y, rows

    def at(self, dx=0, dy=0):
        return (pl.ds(self.x + dx, self.columns), pl.ds(self.y + dy, self.rows))

    def get(self, ref, c, dx=0, dy=0):
        return ref[(c,) + self.at(dx, dy)]

    def put(self, ref, c, values):
        ref[(c,) + self.at()] = values


def tall(x):
    return Block(x, 1, BEGIN[1] - HALO, OWN + 2 * HALO)


def flat(x):
    return Block(x, 2, BEGIN[1], OWN)


def sweep(body, wide, count=2):
    low, high = BEGIN[0], BEGIN[0] + OWN

    def own(i, carry):
        body(flat(low + 2 * i))
        return carry

    def own_tall(x, carry):
        body(tall(x))
        return carry

    def side(i, carry):
        half = count // 2
        body(flat(jnp.where(i < half, low - count + 2 * i, high + 2 * (i - half))))
        return carry

    if wide:
        lax.fori_loop(0, count, side, 0)
        lax.fori_loop(low, high, own_tall, 0)
    else:
        lax.fori_loop(0, OWN // 2, own, 0)


def derivatives(ref, c, block, axes=(0, 1, 2)):
    found = []
    for axis in axes:
        if axis == 2:
            value = block.get(ref, c)
            once = turn(value, 1) - turn(value, -1)
            found.append(8.0 * once - (turn(once, 1) + turn(once, -1)))
        else:
            near, far = [
                block.get(ref, c, *((by, 0) if axis == 0 else (0, by)))
                - block.get(ref, c, *((-by, 0) if axis == 0 else (0, -by)))
                for by in (1, 2)
            ]
            found.append(8.0 * near - far)
    return found


def fluxes(q_ref, f_ref, block):
    q = [block.get(q_ref, c) for c in range(5)]
    inverse = 1.0 / q[0]
    u = [q[1 + j] * inverse for j in range(3)]
    p = (GAMMA - 1.0) * (q[4] - 0.5 * (q[1] * u[0] + q[2] * u[1] + q[3] * u[2]))
    h = q[4] + p
    for d in range(3):
        for j in range(3):
            part = q[1 + j] * u[d]
            block.put(f_ref, 4 * d + j, part + p if j == d else part)
        block.put(f_ref, 4 * d + 3, h * u[d])


def flow_rates(q_ref, f_ref, block):
    rates = []
    for c in range(5):
        f = [(q_ref, 1 + d) if c == 0 else (f_ref, 4 * d + c - 1) for d in range(3)]
        sums = []
        for by in (1, 2):
            ahead, behind = ((by, 0), (0, by)), ((-by, 0), (0, -by))
            flow = [
                block.get(*f[d], *behind[d]) - block.get(*f[d], *ahead[d]) for d in range(2)
            ]
            spread = [
                block.get(q_ref, c, *ahead[d]) + block.get(q_ref, c, *behind[d]) for d in range(2)
            ]
            sums.append((flow[0] + flow[1], spread[0] + spread[1]))
        q, along = block.get(q_ref, c), block.get(*f[2])
        eight, near, far = 8.0 * along, (16.0 * VISCOSITY) * q, VISCOSITY * q
        total = 8.0 * sums[0][0] - sums[1][0] + (16.0 * VISCOSITY) * sums[0][1]
        total -= VISCOSITY * sums[1][1] + (90.0 * VISCOSITY) * q
        total += turn(near - eight, 1) + turn(near + eight, -1)
        total += turn(along - far, 2) - turn(along + far, -2)
        rates.append(total * (1.0 / 12.0))
    return rates


def sound_rates(a_ref, mean_ref, block):
    mean = [block.get(mean_ref, c) for c in range(5)]
    speed = [mean[j] * (1.0 / 12.0) for j in range(3)]
    density = mean[3] * (1.0 / 12.0)
    inverse = (1.0 / 12.0) / mean[3]
    slopes = [derivatives(a_ref, c, block) for c in range(5)]
    carried = [speed[0] * d[0] + speed[1] * d[1] + speed[2] * d[2] for d in slopes]
    divergence = density * (slopes[1][0] + slopes[2][1] + slopes[3][2])
    rates = [-carried[0] - divergence]
    for j in range(3):
        rates.append(-carried[1 + j] - slopes[4][j] * inverse)
    rates.append(-carried[4] - mean[4] * mean[4] * divergence)
    return rates


def lamb(u_ref, block):
    u = [block.get(u_ref, c) * (1.0 / 12.0) for c in range(3)]
    d = [derivatives(u_ref, c, block, tuple(k for k in range(3) if k != c)) for c in range(3)]
    spin = (d[2][1] - d[1][1], d[0][1] - d[2][0], d[1][0] - d[0][0])
    return [
        spin[1] * u[2] - spin[2] * u[1],
        spin[2] * u[0] - spin[0] * u[2],
        spin[0] * u[1] - spin[1] * u[0],
    ]


def kernel(
    nx,
    nr,
    fields,
    mean_flow,
    blocks,
    out,
    own,
    own_mean,
    own_speed,
    start,
    mean,
    speed,
    source,
    odd,
    even,
    flux,
    slope,
    send,
    receive,
    local,
    ready,
):
    sec = lax.axis_index("sec")
    gx = lax.axis_index("gx")
    row = lax.axis_index("row")
    is_flow = sec == 0
    is_sound = sec == 1
    first, last = gx == 0, gx == nx - 1

    def place(section, dx, dy):
        return {
            "sec": section,
            "gx": lax.rem(gx + dx + nx, nx),
            "row": lax.rem(row + dy + nr, nr),
        }

    barrier = pltpu.get_barrier_semaphore()

    def greet(device):
        pl.semaphore_signal(barrier, inc=1, device_id=device, device_id_type=MESH)

    for dx, dy in DIRECTIONS:
        greet(place(sec, dx, dy))

    @pl.when((is_sound & (gx < nx - 1)) | (is_flow & last))
    def _():
        greet(place(1 - sec, 0, 0))

    @pl.when(is_sound & first)
    def _():
        for dy in (-1, 0, 1):
            greet(place(0, -1, dy))

    @pl.when(is_sound & last)
    def _():
        for dy in (-1, 0, 1):
            greet(place(0, 1, dy))

    inner = (slice(None), pl.ds(BEGIN[0], OWN), pl.ds(BEGIN[1], OWN))
    load = pltpu.make_async_copy(fields.at[0], own, local.at[0])
    load.start()
    load_start = pltpu.make_async_copy(fields.at[0], start.at[inner], local.at[1])
    load_start.start()
    load_mean = pltpu.make_async_copy(mean_flow, own_mean, local.at[2])
    load_inner = pltpu.make_async_copy(mean_flow, mean.at[inner], local.at[3])

    @pl.when(is_sound)
    def _():
        load_mean.start()
        load_inner.start()

    load.wait()

    @pl.when(is_flow)
    def _():
        for x in range(OWN):
            inverse = 1.0 / own[0, x]
            for j in range(3):
                own_speed[j, x] = own[1 + j, x] * inverse

    @pl.when(is_sound)
    def _():
        load_mean.wait()

    for found, peers in (
        (is_flow & first, 12),
        (is_flow & (gx > 0) & (gx < nx - 1), 9),
        (is_flow & last, 11),
        (is_sound & (gx < nx - 1), 8),
        (is_sound & last, 9),
    ):

        @pl.when(found)
        def _():
            pl.semaphore_wait(barrier, peers)

    @pl.when(is_sound & last)
    def _():
        pl.semaphore_signal(ready, inc=1, device_id=place(0, 0, 0), device_id_type=MESH)

    def remote(origin, target, index, device):
        return pltpu.make_async_remote_copy(
            src_ref=origin,
            dst_ref=target,
            send_sem=send.at[index],
            recv_sem=receive.at[index],
            device_id=device,
            device_id_type=MESH,
        )

    def copies(section, origin, held, target, base, count=8, width=HALO):
        made = []
        for i in range(count):
            block, middle, slot = parts(DIRECTIONS[i], width)
            made.append(
                remote(
                    origin.at[middle if held else block],
                    target.at[slot],
                    base + i,
                    place(section, *DIRECTIONS[i]),
                )
            )
        return made

    field_copies = copies(sec, own, False, start, FIELD)
    mean_copies = copies(1, own_mean, False, mean, MEAN, count=4, width=2)
    speed_copies = copies(1, speed, True, speed, SPEED)
    around = copies(1, own_speed, False, speed, SPEED)
    stage_copies = copies(sec, even, True, even, STAGE)
    partner_copy = remote(own_speed, speed.at[inner], PARTNER, place(1, 0, 0))
    up = [i for i, d in enumerate(DIRECTIONS) if d[0] == 1]
    down = [i for i, d in enumerate(DIRECTIONS) if d[0] == -1]
    level = [i for i, d in enumerate(DIRECTIONS) if d[0] == 0]

    for copy in field_copies:
        copy.start()

    @pl.when(is_flow & (gx < nx - 1))
    def _():
        partner_copy.start()

    @pl.when(is_flow & first)
    def _():
        for i in down:
            around[i].start()

    @pl.when(is_flow & last)
    def _():
        for i in up:
            around[i].start()
        pl.semaphore_wait(ready, 1)
        partner_copy.start()

    @pl.when(is_sound)
    def _():
        for copy in mean_copies:
            copy.start()

    def advance(rate, prepare):
        prepare(odd, False)

        def second(block):
            for c, k in enumerate(rate(odd, block)):
                block.put(even, c, block.get(start, c) + (0.5 * STEP_DT) * k)
                block.put(slope, c, block.get(slope, c) + 2.0 * k)

        sweep(second, False)
        for copy in stage_copies:
            copy.start()
        for copy in stage_copies:
            copy.wait()
        prepare(even, True)

        def third(block):
            for c, k in enumerate(rate(even, block)):
                block.put(odd, c, block.get(start, c) + STEP_DT * k)
                block.put(slope, c, block.get(slope, c) + 2.0 * k)

        sweep(third, True)
        prepare(odd, False)

        def fourth(block):
            for c, k in enumerate(rate(odd, block)):
                state = block.get(start, c) + (STEP_DT / 6.0) * (block.get(slope, c) + k)
                out[0, c, pl.ds(block.x - BEGIN[0], block.columns)] = state

        sweep(fourth, False)

    load_start.wait()

    @pl.when(is_flow)
    def _():
        for copy in field_copies:
            copy.wait_recv()

        def rate(ref, block):
            return flow_rates(ref, flux, block)

        def prepare(ref, wide):
            low, high = BEGIN[0], BEGIN[0] + OWN
            reach = HALO if wide else 2

            def columns(i, carry):
                fluxes(ref, flux, tall(low - reach + 2 + i))
                return carry

            def ends(i, carry):
                fluxes(ref, flux, flat(jnp.where(i == 0, low - reach, high + reach - 2)))
                return carry

            lax.fori_loop(0, 2, ends, 0)
            lax.fori_loop(0, OWN + 2 * reach - 4, columns, 0)

        prepare(start, True)

        def one(block):
            for c, k in enumerate(rate(start, block)):
                block.put(odd, c, block.get(start, c) + (0.5 * STEP_DT) * k)
                block.put(slope, c, k)

        sweep(one, True)
        advance(rate, prepare)
        partner_copy.wait_send()

    @pl.when(is_sound)
    def _():
        partner_copy.wait_recv()
        for i in level:
            speed_copies[i].start()

        @pl.when(gx < nx - 1)
        def _():
            for i in up:
                speed_copies[i].start()

        @pl.when(gx > 0)
        def _():
            for i in down:
                speed_copies[i].start()

        for copy in field_copies + mean_copies:
            copy.wait_recv()
        load_inner.wait()

        def plain(block):
            for c, k in enumerate(sound_rates(start, mean, block)):
                block.put(slope, c, k)

        sweep(plain, True)
        for copy in speed_copies:
            copy.wait_recv()

        cells = nx * OWN

        def one(block):
            masks = []
            for i in range(block.columns):
                cell = lax.rem(gx * OWN + block.x + i - BEGIN[0] + cells, cells)
                masks.append(blocks[cell // MBLEN].astype(jnp.float32))
            terms = lamb(speed, block)
            for j in range(3):
                for i in range(block.columns):
                    column = Block(block.x + i, 1, block.y, block.rows)
                    column.put(source, j, masks[i] * terms[j][i : i + 1])
            for c in range(5):
                k = block.get(slope, c)
                if 1 <= c <= 3:
                    k = k - block.get(source, c - 1)
                    block.put(slope, c, k)
                block.put(odd, c, block.get(start, c) + (0.5 * STEP_DT) * k)

        sweep(one, True)

        def rate(ref, block):
            rates = sound_rates(ref, mean, block)
            return [
                k - block.get(source, c - 1) if 1 <= c <= 3 else k for c, k in enumerate(rates)
            ]

        advance(rate, lambda ref, wide: None)
        for i in level:
            speed_copies[i].wait_send()

        @pl.when(gx < nx - 1)
        def _():
            for i in up:
                speed_copies[i].wait_send()

        @pl.when(gx > 0)
        def _():
            for i in down:
                speed_copies[i].wait_send()

        for copy in mean_copies:
            copy.wait_send()

    for copy in field_copies:
        copy.wait_send()

    @pl.when(is_flow & last)
    def _():
        for i in up:
            around[i].wait_send()

    @pl.when(is_flow & first)
    def _():
        for i in down:
            around[i].wait_send()


def solution(mesh):
    nx, nr = mesh.shape["gx"], mesh.shape["row"]

    def local(fields, mean_flow, source_blocks):
        return pl.pallas_call(
            functools.partial(kernel, nx, nr),
            out_shape=jax.ShapeDtypeStruct(fields.shape, jnp.float32),
            in_specs=[
                pl.BlockSpec(memory_space=pl.ANY),
                pl.BlockSpec(memory_space=pl.ANY),
                pl.BlockSpec(memory_space=pltpu.SMEM),
            ],
            out_specs=pl.BlockSpec(memory_space=pltpu.VMEM),
            scratch_shapes=[
                pltpu.VMEM((5, OWN, OWN, 128), jnp.float32),
                pltpu.VMEM((5, OWN, OWN, 128), jnp.float32),
                pltpu.VMEM((3, OWN, OWN, 128), jnp.float32),
                pltpu.VMEM((5,) + WINDOW, jnp.float32),
                pltpu.VMEM((5,) + WINDOW, jnp.float32),
                pltpu.VMEM((3,) + WINDOW, jnp.float32),
                pltpu.VMEM((3,) + WINDOW, jnp.float32),
                pltpu.VMEM((5,) + WINDOW, jnp.float32),
                pltpu.VMEM((5,) + WINDOW, jnp.float32),
                pltpu.VMEM((12,) + WINDOW, jnp.float32),
                pltpu.VMEM((5,) + WINDOW, jnp.float32),
                pltpu.SemaphoreType.DMA((SEMAPHORES,)),
                pltpu.SemaphoreType.DMA((SEMAPHORES,)),
                pltpu.SemaphoreType.DMA((4,)),
                pltpu.SemaphoreType.REGULAR,
            ],
            compiler_params=pltpu.CompilerParams(collective_id=0, has_side_effects=True),
        )(fields, mean_flow, source_blocks)

    return jax.shard_map(
        local,
        mesh=mesh,
        in_specs=(P("sec", None, "gx", "row", None), P(None, "gx", "row", None), P()),
        out_specs=P("sec", None, "gx", "row", None),
        check_vma=False,
    )
```

time: 46.5 us -> 43.1 us (0.927); the launches traced: 46.3 us -> 42.4 us
  Pallas kernels: 44.7 us -> 40.8 us
    pallas_call x1, Pallas kernels: 44.7 us -> 40.8 us  [local(): pl.pallas_call(functools.partial(kernel, nx, nr), out_shape=jax.ShapeDtyp...]
where the time goes in v3:
time: 43.1 us; the launch traced here: 42.4 us
  Pallas kernels  40.8 us (95%)
  local copies, waits for them, and re-layouts  1.59 us (4%)
    pallas_call x1, Pallas kernels, local(): pl.pallas_call(functools.partial(kernel, nx, nr), out_shape=jax.ShapeDtyp...  40.8 us
    unnamed x1, local copies, waits for them, and re-layouts  1.59 us

profile of v3, /device:TPU:1, one launch (start us, length us, event | category | flops | bytes accessed | tf_op | source)
XLA Modules:
  0.0 42.4 jit_solution(12291351906346666249)
XLA Ops:
  0.0 40.8 %shard_map.37 = f32[1,5,8,8,128]{4,3,2,1,0:T(8,128)} custom-call(f32[1,5,8,8,128]{4,3,2,1,0:T(8,128)} %fields.1, f32[5,8,8,128]{3,2,1,0:T(8,128)} %mean_flow.1, s32[64]{0:T(128)} %blocks.1), custom_call_target="tpu_custom_call" | custom-call | tf_op jit(solution)/shard_map/pallas_call | solution.py:491
  40.8 1.6 %copy.5 = f32[1,5,8,8,128]{4,3,2,1,0:T(8,128)} copy(f32[1,5,8,8,128]{4,3,2,1,0:T(8,128)} %shard_map.37) | data formatting | bytes 327680

commit v4 on v3

--- a/solution.py
+++ b/solution.py
@@ -178,8 +178,9 @@
     nr,
     fields,
     mean_flow,
-    blocks,
+    all_blocks,
     out,
+    last_slope,
     own,
     own_mean,
     own_speed,
@@ -195,6 +196,7 @@
     receive,
     local,
     ready,
+    blocks,
 ):
     sec = lax.axis_index("sec")
     gx = lax.axis_index("gx")
@@ -238,12 +240,14 @@
     load_start = pltpu.make_async_copy(fields.at[0], start.at[inner], local.at[1])
     load_start.start()
     load_mean = pltpu.make_async_copy(mean_flow, own_mean, local.at[2])
+    load_blocks = pltpu.make_async_copy(all_blocks, blocks, local.at[4])
     load_inner = pltpu.make_async_copy(mean_flow, mean.at[inner], local.at[3])
 
     @pl.when(is_sound)
     def _():
         load_mean.start()
         load_inner.start()
+        load_blocks.start()
 
     load.wait()
 
@@ -357,8 +361,9 @@
 
         def fourth(block):
             for c, k in enumerate(rate(odd, block)):
-                state = block.get(start, c) + (STEP_DT / 6.0) * (block.get(slope, c) + k)
-                out[0, c, pl.ds(block.x - BEGIN[0], block.columns)] = state
+                columns = pl.ds(block.x - BEGIN[0], block.columns)
+                out[0, c, columns] = block.get(start, c) + (STEP_DT / 6.0) * block.get(slope, c)
+                last_slope[0, c, columns] = k
 
         sweep(fourth, False)
 
@@ -417,6 +422,7 @@
         for copy in field_copies + mean_copies:
             copy.wait_recv()
         load_inner.wait()
+        load_blocks.wait()
 
         def plain(block):
             for c, k in enumerate(sound_rates(start, mean, block)):
@@ -488,15 +494,18 @@
     nx, nr = mesh.shape["gx"], mesh.shape["row"]
 
     def local(fields, mean_flow, source_blocks):
-        return pl.pallas_call(
+        fields = pltpu.with_memory_space_constraint(fields, pltpu.HBM)
+        mean_flow = pltpu.with_memory_space_constraint(mean_flow, pltpu.HBM)
+        source_blocks = pltpu.with_memory_space_constraint(source_blocks, pltpu.HBM)
+        state, last_slope = pl.pallas_call(
             functools.partial(kernel, nx, nr),
-            out_shape=jax.ShapeDtypeStruct(fields.shape, jnp.float32),
+            out_shape=[jax.ShapeDtypeStruct(fields.shape, jnp.float32)] * 2,
             in_specs=[
-                pl.BlockSpec(memory_space=pl.ANY),
-                pl.BlockSpec(memory_space=pl.ANY),
-                pl.BlockSpec(memory_space=pltpu.SMEM),
+                pl.BlockSpec(memory_space=pltpu.HBM),
+                pl.BlockSpec(memory_space=pltpu.HBM),
+                pl.BlockSpec(memory_space=pltpu.HBM),
             ],
-            out_specs=pl.BlockSpec(memory_space=pltpu.VMEM),
+            out_specs=[pl.BlockSpec(memory_space=pltpu.VMEM)] * 2,
             scratch_shapes=[
                 pltpu.VMEM((5, OWN, OWN, 128), jnp.float32),
                 pltpu.VMEM((5, OWN, OWN, 128), jnp.float32),
@@ -511,11 +520,15 @@
                 pltpu.VMEM((5,) + WINDOW, jnp.float32),
                 pltpu.SemaphoreType.DMA((SEMAPHORES,)),
                 pltpu.SemaphoreType.DMA((SEMAPHORES,)),
-                pltpu.SemaphoreType.DMA((4,)),
+                pltpu.SemaphoreType.DMA((5,)),
                 pltpu.SemaphoreType.REGULAR,
+                pltpu.SMEM(source_blocks.shape, jnp.int32),
             ],
-            compiler_params=pltpu.CompilerParams(collective_id=0, has_side_effects=True),
+            compiler_params=pltpu.CompilerParams(
+                collective_id=0, has_side_effects=True, vmem_limit_bytes=16 * 1024 * 1024
+            ),
         )(fields, mean_flow, source_blocks)
+        return state + (STEP_DT / 6.0) * last_slope
 
     return jax.shard_map(
         local,

time: 43.1 us -> 40.8 us (0.947)
  local copies, waits for them, and re-layouts: 1.59 us -> 0 us
  Pallas kernels: 40.8 us -> 39.5 us
  other arithmetic: 0 us -> 0.69 us
    unnamed x1 -> x0, local copies, waits for them, and re-layouts: 1.59 us -> none
    pallas_call x1, Pallas kernels: 40.8 us -> 39.5 us  [local(): pl.pallas_call(functools.partial(kernel, nx, nr), out_shape=[jax.ShapeDty...]
    add x0 -> x1, other arithmetic: none -> 0.69 us  [local(): return state + STEP_DT / 6.0 * last_slope]
where the time goes in v4:
time: 40.8 us; the launch traced here: 40.2 us
  Pallas kernels  39.5 us (97%)
  other arithmetic  0.69 us (2%)
    pallas_call x1, Pallas kernels, local(): pl.pallas_call(functools.partial(kernel, nx, nr), out_shape=[jax.ShapeDty...  39.5 us

profile of v4, /device:TPU:1, one launch (start us, length us, event | category | flops | bytes accessed | tf_op | source)
XLA Modules:
  0.0 40.2 jit_solution(9969225886168134169)
XLA Ops:
  0.0 39.5 %shard_map.37 = (f32[1,5,8,8,128]{4,3,2,1,0:T(8,128)S(1)}, f32[1,5,8,8,128]{4,3,2,1,0:T(8,128)S(1)}) custom-call(f32[1,5,8,8,128]{4,3,2,1,0:T(8,128)} %fields.1, f32[5,8,8,128]{3,2,1,0:T(8,128)} %mean_flow.1, s32[64]{0:T(128)} %all_blocks.1), custom_call_target="tpu_custom_call" | custom-call | tf_op jit(solution)/shard_map/pallas_call | solution.py:500
  39.5 0.7 %multiply_add_fusion = f32[1,5,8,8,128]{4,3,2,1,0:T(8,128)} fusion(f32[1,5,8,8,128]{4,3,2,1,0:T(8,128)S(1)} %get-tuple-element.7, f32[1,5,8,8,128]{4,3,2,1,0:T(8,128)S(1)} %get-tuple-element.8), kind=kLoop, calls=%fused_computation | loop fusion | flops 81920 | bytes 491520 | tf_op jit(solution)/shard_map/add | solution.py:531

commit v5 on v4

--- a/solution.py
+++ b/solution.py
@@ -70,27 +70,36 @@
     return Block(x, 2, BEGIN[1], OWN)
 
 
-def sweep(body, wide, count=2):
-    low, high = BEGIN[0], BEGIN[0] + OWN
-
+LOW, HIGH = BEGIN[0], BEGIN[0] + OWN
+
+
+def sweep(body):
     def own(i, carry):
-        body(flat(low + 2 * i))
+        body(flat(LOW + 2 * i))
         return carry
 
-    def own_tall(x, carry):
+    lax.fori_loop(0, OWN // 2, own, 0)
+
+
+def sweep_middle(body):
+    def middle(x, carry):
         body(tall(x))
         return carry
 
+    lax.fori_loop(LOW + 2, HIGH - 2, middle, 0)
+
+
+def sweep_rest(body):
+    def edge(i, carry):
+        body(tall(jnp.where(i < 2, LOW + i, HIGH - 4 + i)))
+        return carry
+
     def side(i, carry):
-        half = count // 2
-        body(flat(jnp.where(i < half, low - count + 2 * i, high + 2 * (i - half))))
+        body(flat(jnp.where(i == 0, LOW - 2, HIGH)))
         return carry
 
-    if wide:
-        lax.fori_loop(0, count, side, 0)
-        lax.fori_loop(low, high, own_tall, 0)
-    else:
-        lax.fori_loop(0, OWN // 2, own, 0)
+    lax.fori_loop(0, 4, edge, 0)
+    lax.fori_loop(0, 2, side, 0)
 
 
 def derivatives(ref, c, block, axes=(0, 1, 2)):
@@ -337,27 +346,31 @@
             copy.start()
 
     def advance(rate, prepare):
-        prepare(odd, False)
+        prepare(odd, 0)
 
         def second(block):
             for c, k in enumerate(rate(odd, block)):
                 block.put(even, c, block.get(start, c) + (0.5 * STEP_DT) * k)
                 block.put(slope, c, block.get(slope, c) + 2.0 * k)
 
-        sweep(second, False)
+        sweep(second)
         for copy in stage_copies:
             copy.start()
-        for copy in stage_copies:
-            copy.wait()
-        prepare(even, True)
 
         def third(block):
             for c, k in enumerate(rate(even, block)):
                 block.put(odd, c, block.get(start, c) + STEP_DT * k)
                 block.put(slope, c, block.get(slope, c) + 2.0 * k)
 
-        sweep(third, True)
-        prepare(odd, False)
+        for i in level:
+            stage_copies[i].wait()
+        prepare(even, 1)
+        sweep_middle(third)
+        for i in up + down:
+            stage_copies[i].wait()
+        prepare(even, 2)
+        sweep_rest(third)
+        prepare(odd, 0)
 
         def fourth(block):
             for c, k in enumerate(rate(odd, block)):
@@ -365,41 +378,49 @@
                 out[0, c, columns] = block.get(start, c) + (STEP_DT / 6.0) * block.get(slope, c)
                 last_slope[0, c, columns] = k
 
-        sweep(fourth, False)
+        sweep(fourth)
 
     load_start.wait()
 
     @pl.when(is_flow)
     def _():
-        for copy in field_copies:
-            copy.wait_recv()
-
         def rate(ref, block):
             return flow_rates(ref, flux, block)
 
-        def prepare(ref, wide):
-            low, high = BEGIN[0], BEGIN[0] + OWN
-            reach = HALO if wide else 2
-
-            def columns(i, carry):
-                fluxes(ref, flux, tall(low - reach + 2 + i))
+        def prepare(ref, step):
+            def columns(x, carry):
+                fluxes(ref, flux, tall(x))
                 return carry
 
+            def beside(i, carry):
+                fluxes(ref, flux, tall(jnp.where(i < 2, LOW - 2 + i, HIGH - 2 + i)))
+                return carry
+
             def ends(i, carry):
-                fluxes(ref, flux, flat(jnp.where(i == 0, low - reach, high + reach - 2)))
+                reach = 2 if step == 0 else HALO
+                fluxes(ref, flux, flat(jnp.where(i == 0, LOW - reach, HIGH + reach - 2)))
                 return carry
 
-            lax.fori_loop(0, 2, ends, 0)
-            lax.fori_loop(0, OWN + 2 * reach - 4, columns, 0)
-
-        prepare(start, True)
+            if step < 2:
+                lax.fori_loop(LOW, HIGH, columns, 0)
+            if step == 2:
+                lax.fori_loop(0, 4, beside, 0)
+            if step != 1:
+                lax.fori_loop(0, 2, ends, 0)
 
         def one(block):
             for c, k in enumerate(rate(start, block)):
                 block.put(odd, c, block.get(start, c) + (0.5 * STEP_DT) * k)
                 block.put(slope, c, k)
 
-        sweep(one, True)
+        for i in level:
+            field_copies[i].wait_recv()
+        prepare(start, 1)
+        sweep_middle(one)
+        for i in up + down:
+            field_copies[i].wait_recv()
+        prepare(start, 2)
+        sweep_rest(one)
         advance(rate, prepare)
         partner_copy.wait_send()
 
@@ -428,9 +449,8 @@
             for c, k in enumerate(sound_rates(start, mean, block)):
                 block.put(slope, c, k)
 
-        sweep(plain, True)
-        for copy in speed_copies:
-            copy.wait_recv()
+        sweep_middle(plain)
+        sweep_rest(plain)
 
         cells = nx * OWN
 
@@ -451,7 +471,12 @@
                     block.put(slope, c, k)
                 block.put(odd, c, block.get(start, c) + (0.5 * STEP_DT) * k)
 
-        sweep(one, True)
+        for i in level:
+            speed_copies[i].wait_recv()
+        sweep_middle(one)
+        for i in up + down:
+            speed_copies[i].wait_recv()
+        sweep_rest(one)
 
         def rate(ref, block):
             rates = sound_rates(ref, mean, block)
@@ -459,7 +484,7 @@
                 k - block.get(source, c - 1) if 1 <= c <= 3 else k for c, k in enumerate(rates)
             ]
 
-        advance(rate, lambda ref, wide: None)
+        advance(rate, lambda ref, step: None)
         for i in level:
             speed_copies[i].wait_send()
 

time: 40.8 us -> 39.5 us (0.968)
  Pallas kernels: 39.5 us -> 38.3 us
    pallas_call x1, Pallas kernels: 39.5 us -> 38.3 us  [local(): pl.pallas_call(functools.partial(kernel, nx, nr), out_shape=[jax.ShapeDty...]
where the time goes in v5:
time: 39.5 us; the launch traced here: 39 us
  Pallas kernels  38.3 us (97%)
  other arithmetic  0.69 us (2%)
    pallas_call x1, Pallas kernels, local(): pl.pallas_call(functools.partial(kernel, nx, nr), out_shape=[jax.ShapeDty...  38.3 us

profile of v5, /device:TPU:1, one launch (start us, length us, event | category | flops | bytes accessed | tf_op | source)
XLA Modules:
  0.0 39.0 jit_solution(5842830687423141870)
XLA Ops:
  0.0 38.3 %shard_map.37 = (f32[1,5,8,8,128]{4,3,2,1,0:T(8,128)S(1)}, f32[1,5,8,8,128]{4,3,2,1,0:T(8,128)S(1)}) custom-call(f32[1,5,8,8,128]{4,3,2,1,0:T(8,128)} %fields.1, f32[5,8,8,128]{3,2,1,0:T(8,128)} %mean_flow.1, s32[64]{0:T(128)} %all_blocks.1), custom_call_target="tpu_custom_call" | custom-call | tf_op jit(solution)/shard_map/pallas_call | solution.py:525
  38.3 0.7 %multiply_add_fusion = f32[1,5,8,8,128]{4,3,2,1,0:T(8,128)} fusion(f32[1,5,8,8,128]{4,3,2,1,0:T(8,128)S(1)} %get-tuple-element.7, f32[1,5,8,8,128]{4,3,2,1,0:T(8,128)S(1)} %get-tuple-element.8), kind=kLoop, calls=%fused_computation | loop fusion | flops 81920 | bytes 491520 | tf_op jit(solution)/shard_map/add | solution.py:556

commit v6 on v5

--- a/solution.py
+++ b/solution.py
@@ -78,7 +78,7 @@
         body(flat(LOW + 2 * i))
         return carry
 
-    lax.fori_loop(0, OWN // 2, own, 0)
+    lax.fori_loop(0, OWN // 2, own, 0, unroll=2)
 
 
 def sweep_middle(body):
@@ -86,7 +86,7 @@
         body(tall(x))
         return carry
 
-    lax.fori_loop(LOW + 2, HIGH - 2, middle, 0)
+    lax.fori_loop(LOW + 2, HIGH - 2, middle, 0, unroll=2)
 
 
 def sweep_rest(body):
@@ -98,8 +98,8 @@
         body(flat(jnp.where(i == 0, LOW - 2, HIGH)))
         return carry
 
-    lax.fori_loop(0, 4, edge, 0)
-    lax.fori_loop(0, 2, side, 0)
+    lax.fori_loop(0, 4, edge, 0, unroll=2)
+    lax.fori_loop(0, 2, side, 0, unroll=2)
 
 
 def derivatives(ref, c, block, axes=(0, 1, 2)):
@@ -402,11 +402,11 @@
                 return carry
 
             if step < 2:
-                lax.fori_loop(LOW, HIGH, columns, 0)
+                lax.fori_loop(LOW, HIGH, columns, 0, unroll=2)
             if step == 2:
-                lax.fori_loop(0, 4, beside, 0)
+                lax.fori_loop(0, 4, beside, 0, unroll=2)
             if step != 1:
-                lax.fori_loop(0, 2, ends, 0)
+                lax.fori_loop(0, 2, ends, 0, unroll=2)
 
         def one(block):
             for c, k in enumerate(rate(start, block)):
@@ -427,8 +427,6 @@
     @pl.when(is_sound)
     def _():
         partner_copy.wait_recv()
-        for i in level:
-            speed_copies[i].start()
 
         @pl.when(gx < nx - 1)
         def _():
@@ -439,6 +437,9 @@
         def _():
             for i in down:
                 speed_copies[i].start()
+
+        for i in level:
+            speed_copies[i].start()
 
         for copy in field_copies + mean_copies:
             copy.wait_recv()

time: 39.5 us -> 38.1 us (0.965); the launches traced: 39 us -> 38 us
  Pallas kernels: 38.3 us -> 37.3 us
    pallas_call x1, Pallas kernels: 38.3 us -> 37.3 us  [local(): pl.pallas_call(functools.partial(kernel, nx, nr), out_shape=[jax.ShapeDty...]
where the time goes in v6:
time: 38.1 us; the launch traced here: 38 us
  Pallas kernels  37.3 us (98%)
  other arithmetic  0.69 us (2%)
    pallas_call x1, Pallas kernels, local(): pl.pallas_call(functools.partial(kernel, nx, nr), out_shape=[jax.ShapeDty...  37.3 us

profile of v6, /device:TPU:1, one launch (start us, length us, event | category | flops | bytes accessed | tf_op | source)
XLA Modules:
  0.0 38.0 jit_solution(1847152405277041147)
XLA Ops:
  0.0 37.3 %shard_map.37 = (f32[1,5,8,8,128]{4,3,2,1,0:T(8,128)S(1)}, f32[1,5,8,8,128]{4,3,2,1,0:T(8,128)S(1)}) custom-call(f32[1,5,8,8,128]{4,3,2,1,0:T(8,128)} %fields.1, f32[5,8,8,128]{3,2,1,0:T(8,128)} %mean_flow.1, s32[64]{0:T(128)} %all_blocks.1), custom_call_target="tpu_custom_call" | custom-call | tf_op jit(solution)/shard_map/pallas_call | solution.py:526
  37.3 0.7 %multiply_add_fusion = f32[1,5,8,8,128]{4,3,2,1,0:T(8,128)} fusion(f32[1,5,8,8,128]{4,3,2,1,0:T(8,128)S(1)} %get-tuple-element.7, f32[1,5,8,8,128]{4,3,2,1,0:T(8,128)S(1)} %get-tuple-element.8), kind=kLoop, calls=%fused_computation | loop fusion | flops 81920 | bytes 491520 | tf_op jit(solution)/shard_map/add | solution.py:557
